TPU v7x, 32 devices: a whole 2x2x4 slice. The times are simulated.
32 devices in a mesh: wa: 4 (over z), ha: 8 (over y, x, core).
Axes of the slice: x: 2, y: 2, z: 4, core: 2. Of those that a mesh axis runs over, the one named last changes fastest.
Arguments:
- tokens: bfloat16 [1024, 16384], P('ha', 'wa'), may hold values from -6 to 6
- gain_attn: bfloat16 [16384], P('wa'), may hold values from 0.25 to 1.75
- w_query: bfloat16 [16384, 16384], P('wa', 'ha'), may hold values from -0.046875 to 0.046875, as said below
- w_key: bfloat16 [16384, 1024], P('wa'), may hold values from -1.171875 to 1.171875, as said below
- w_value: bfloat16 [16384, 1024], P('wa'), may hold values from -0.046875 to 0.046875
- w_out: bfloat16 [16384, 16384], P('ha', 'wa'), may hold values from -0.1875 to 0.1875
- gain_ffn: bfloat16 [16384], P('wa'), may hold values from 0.25 to 1.75
- segment_ids: int32 [1024], replicated, may hold values from 0 to 31, never falling along the last dimension, each value on 1 to 256 neighbouring positions
Outputs:
- residual_out: bfloat16 [1024, 16384], P('ha', 'wa')
- ffn_input: bfloat16 [1024, 16384], P('ha', 'wa')
Inputs may be any that keep to these rules, and one draw needn't show every extreme that they name: `w_query`: entries scaled by 16384 ** -0.5. `w_key`: entries scaled by 16384 ** -0.5. `segment_ids`: segment ids never fall along the tokens; each prompt has 1 to 256 tokens and one has exactly 256.
All inputs are finite; a program needn't handle non-finite values.
Results may differ from a plain program's by a relative error of at most 0.00675.
The roundings to bfloat16 on the way count: a program that leaves them out, or rounds other values in their place, can miss the bound.
Values may be sent and summed in bfloat16 or wider, within the bound.
A program may use at most 192 MiB of HBM per device.

v0:
```python
import functools

import jax
import jax.numpy as jnp
from jax import lax
from jax.experimental import pallas as pl
from jax.experimental.pallas import tpu as pltpu
from jax.sharding import PartitionSpec as P

KVH = 8
HD = 128
WINDOW = 256


EPS = 1e-05


def rope_tables(position):
    half = HD // 2
    inverse = 500000.0 ** (-(jnp.arange(half, dtype=jnp.float32) * 2.0 / HD))
    angle = position[:, None] * inverse[None, :]
    return (jnp.cos(angle), jnp.sin(angle))


def rotate(values, cosine, sine):
    half = values.shape[-1] // 2
    first = values[..., :half]
    second = values[..., half:]
    cosine = cosine[:, None, :]
    sine = sine[:, None, :]
    return jnp.concatenate(
        [first * cosine - second * sine, second * cosine + first * sine], axis=-1
    )


SKEW = 3


def greet_peers(n):
    me = lax.axis_index("wa")
    barrier = pltpu.get_barrier_semaphore()
    for d in range(1, n):
        pl.semaphore_signal(
            barrier,
            inc=1,
            device_id={"wa": lax.rem(me + d, n)},
            device_id_type=pl.DeviceIdType.MESH,
        )
    pl.semaphore_wait(barrier, n - 1)


def send_to(src, dst, send_sem, recv_sem, peer):
    return pltpu.make_async_remote_copy(
        src_ref=src,
        dst_ref=dst,
        send_sem=send_sem,
        recv_sem=recv_sem,
        device_id={"wa": peer},
        device_id_type=pl.DeviceIdType.MESH,
    )


def peer_copies(n, x_ref, land, sems):
    me = lax.axis_index("wa")
    return [
        send_to(x_ref, land.at[d - 1], sems.at[0, d - 1], sems.at[1, d - 1], lax.rem(me + d, n))
        for d in range(1, n)
    ]


def peer_sum_kernel(n, x_ref, o_ref, land, sems):
    greet_peers(n)
    copies = peer_copies(n, x_ref, land, sems)
    for copy in copies:
        copy.start()
    for copy in copies:
        copy.wait()
    total = x_ref[...]
    for d in range(n - 1):
        total = total + land[d]
    o_ref[...] = total


def peer_sum(x, n):
    vmem = pl.BlockSpec(memory_space=pltpu.VMEM)
    return pl.pallas_call(
        functools.partial(peer_sum_kernel, n),
        out_shape=jax.ShapeDtypeStruct(x.shape, x.dtype),
        in_specs=[vmem],
        out_specs=vmem,
        scratch_shapes=[
            pltpu.VMEM((n - 1,) + x.shape, x.dtype),
            pltpu.SemaphoreType.DMA((2, n - 1)),
        ],
        compiler_params=pltpu.CompilerParams(
            collective_id=2, has_side_effects=True, vmem_limit_bytes=4 << 20
        ),
    )(x)


def reduce_kernel(
    n, nc, half, window, q_ref, kv_ref, sq_ref, qo, kvo, sqo,
    rq, rkv, lq, lkv, lsq, rqs, rks, lqs, lks, sqs,
):
    me = lax.axis_index("wa")
    last = n - 1
    right = jnp.minimum(me + 1, last)
    left = jnp.maximum(me - 1, 0)
    cq = half // nc
    cw = (half + window) // nc
    greet_peers(n)
    small = peer_copies(n, sq_ref, lsq, sqs)
    for copy in small:
        copy.start()
    kvo[pl.ds(0, window), :] = jnp.zeros((window, kvo.shape[1]), kvo.dtype)

    def rows(base, j, size):
        return pl.ds(pl.multiple_of(base + j * size, 8), size)

    def right_copy(j, first_hop):
        own, wide = rows(0, j, cq), rows(0, j, cw)
        if first_hop:
            src, src_kv = q_ref.at[rows(half, j, cq)], kv_ref.at[rows(half - window, j, cw)]
        else:
            src, src_kv = rq.at[own], rkv.at[wide]
        return (
            send_to(src, rq.at[own], rqs.at[0, j], rqs.at[1, j], right),
            send_to(src_kv, rkv.at[wide], rks.at[0, j], rks.at[1, j], right),
        )

    def left_copy(j, first_hop):
        own = rows(0, j, cq)
        src, src_kv = (q_ref, kv_ref) if first_hop else (lq, lkv)
        return (
            send_to(src.at[own], lq.at[own], lqs.at[0, j], lqs.at[1, j], left),
            send_to(src_kv.at[own], lkv.at[own], lks.at[0, j], lks.at[1, j], left),
        )

    @pl.loop(0, nc + SKEW * last)
    def _(s):
        j = s - SKEW * me
        i = s - SKEW * (last - me)
        right_on = (j >= 0) & (j < nc)
        left_on = (i >= 0) & (i < nc)

        @pl.when(right_on & (me > 0))
        def _():
            for copy in right_copy(j, False):
                copy.wait_recv()
            own, wide = rows(0, j, cq), rows(0, j, cw)
            rq[own, :] = rq[own, :] + q_ref[rows(half, j, cq), :]
            rkv[wide, :] = rkv[wide, :] + kv_ref[rows(half - window, j, cw), :]

        @pl.when(left_on & (me < last))
        def _():
            for copy in left_copy(i, False):
                copy.wait_recv()
            own = rows(0, i, cq)
            lq[own, :] = lq[own, :] + q_ref[own, :]
            lkv[own, :] = lkv[own, :] + kv_ref[own, :]

        @pl.when(right_on & (me == 0))
        def _():
            for copy in right_copy(j, True):
                copy.start()

        @pl.when(left_on & (me == last))
        def _():
            for copy in left_copy(i, True):
                copy.start()

        @pl.when(right_on & (me > 0) & (me < last))
        def _():
            for copy in right_copy(j, False):
                copy.start()

        @pl.when(left_on & (me > 0) & (me < last))
        def _():
            for copy in left_copy(i, False):
                copy.start()

        @pl.when(right_on & (me == last))
        def _():
            own, wide = rows(0, j, cq), rows(0, j, cw)
            qo[own, :] = rq[own, :]
            kvo[wide, :] = rkv[wide, :]

        @pl.when(left_on & (me < last))
        def _():
            own = rows(0, i, cq)
            qo[own, :] = lq[own, :]
            kvo[rows(window, i, cq), :] = lkv[own, :]

    @pl.loop(0, nc)
    def _(j):
        @pl.when(me < last)
        def _():
            for copy in right_copy(j, False):
                copy.wait_send()

        @pl.when(me > 0)
        def _():
            for copy in left_copy(j, False):
                copy.wait_send()

    for copy in small:
        copy.wait()
    total = sq_ref[...]
    for d in range(n - 1):
        total = total + lsq[d]
    sqo[...] = total


def reduce_to_ends(q_part, kv_part, row_sq, n, window):
    rows, cols = q_part.shape
    kv_cols = kv_part.shape[1]
    half = rows // 2
    nc = half // 16
    vmem = pl.BlockSpec(memory_space=pltpu.VMEM)
    f32 = jnp.float32
    pair = pltpu.SemaphoreType.DMA((2, nc))
    return pl.pallas_call(
        functools.partial(reduce_kernel, n, nc, half, window),
        out_shape=(
            jax.ShapeDtypeStruct((half, cols), f32),
            jax.ShapeDtypeStruct((half + window, kv_cols), f32),
            jax.ShapeDtypeStruct(row_sq.shape, f32),
        ),
        in_specs=[vmem] * 3,
        out_specs=(vmem,) * 3,
        scratch_shapes=[
            pltpu.VMEM((half, cols), f32),
            pltpu.VMEM((half + window, kv_cols), f32),
            pltpu.VMEM((half, cols), f32),
            pltpu.VMEM((half, kv_cols), f32),
            pltpu.VMEM((n - 1,) + row_sq.shape, f32),
            pair,
            pair,
            pair,
            pair,
            pltpu.SemaphoreType.DMA((2, n - 1)),
        ],
        compiler_params=pltpu.CompilerParams(
            collective_id=0, has_side_effects=True, vmem_limit_bytes=40 << 20
        ),
    )(q_part, kv_part, row_sq)


def spread_kernel(n, nc, half, x_ref, o_ref, rs, ls):
    me = lax.axis_index("wa")
    last = n - 1
    right = jnp.minimum(me + 1, last)
    left = jnp.maximum(me - 1, 0)
    size = half // nc
    greet_peers(n)

    def rows(base, j):
        return pl.ds(pl.multiple_of(base + j * size, 16), size)

    def right_copy(j, first_hop):
        at = rows(0, j)
        src = x_ref if first_hop else o_ref
        return send_to(src.at[at], o_ref.at[at], rs.at[0, j], rs.at[1, j], right)

    def left_copy(j, first_hop):
        at = rows(half, j)
        src = x_ref.at[rows(0, j)] if first_hop else o_ref.at[at]
        return send_to(src, o_ref.at[at], ls.at[0, j], ls.at[1, j], left)

    @pl.loop(0, nc + SKEW * last)
    def _(s):
        j = s - SKEW * me
        i = s - SKEW * (last - me)
        right_on = (j >= 0) & (j < nc)
        left_on = (i >= 0) & (i < nc)

        @pl.when(right_on & (me == 0))
        def _():
            right_copy(j, True).start()
            o_ref[rows(0, j), :] = x_ref[rows(0, j), :]

        @pl.when(left_on & (me == last))
        def _():
            left_copy(i, True).start()
            o_ref[rows(half, i), :] = x_ref[rows(0, i), :]

        @pl.when(right_on & (me > 0))
        def _():
            right_copy(j, False).wait_recv()

        @pl.when(right_on & (me > 0) & (me < last))
        def _():
            right_copy(j, False).start()

        @pl.when(left_on & (me < last))
        def _():
            left_copy(i, False).wait_recv()

        @pl.when(left_on & (me > 0) & (me < last))
        def _():
            left_copy(i, False).start()

    @pl.loop(0, nc)
    def _(j):
        @pl.when(me < last)
        def _():
            right_copy(j, False).wait_send()

        @pl.when(me > 0)
        def _():
            left_copy(j, False).wait_send()


def spread_from_ends(x, n):
    half, cols = x.shape
    nc = half // 16
    vmem = pl.BlockSpec(memory_space=pltpu.VMEM)
    pair = pltpu.SemaphoreType.DMA((2, nc))
    return pl.pallas_call(
        functools.partial(spread_kernel, n, nc, half),
        out_shape=jax.ShapeDtypeStruct((2 * half, cols), x.dtype),
        in_specs=[vmem],
        out_specs=vmem,
        scratch_shapes=[pair, pair],
        compiler_params=pltpu.CompilerParams(
            collective_id=1, has_side_effects=True, vmem_limit_bytes=16 << 20
        ),
    )(x)


def attend(queries, key_head, value_head, segment_ids, first):
    q_rows = queries.shape[0]
    size = min(WINDOW, q_rows)
    segment_pad = jnp.pad(segment_ids, (WINDOW, 0), constant_values=-1)
    outs = []
    for at in range(0, q_rows, size):
        start = first + at
        query = queries[at : at + size]
        key = key_head[at : at + size + WINDOW]
        value = value_head[at : at + size + WINDOW]
        k_segment = lax.dynamic_slice_in_dim(segment_pad, start, size + WINDOW, 0)
        q_segment = lax.dynamic_slice_in_dim(segment_ids, start, size, 0)
        k_at = jnp.arange(size + WINDOW, dtype=jnp.int32) - WINDOW
        q_at = jnp.arange(size, dtype=jnp.int32)
        allowed = (q_segment[:, None] == k_segment[None, :]) & (k_at[None, :] <= q_at[:, None])
        allowed = allowed & (k_at + start >= 0)[None, :]
        scores = jnp.einsum(
            "thd,sd->hts", query, key, preferred_element_type=jnp.float32
        ) * HD ** (-0.5)
        scores = jnp.where(allowed[None], scores, -1e30)
        peak = jnp.max(scores, axis=-1, keepdims=True)
        expo = jnp.where(allowed[None], jnp.exp(scores - peak), 0.0)
        weights = (expo / jnp.sum(expo, axis=-1, keepdims=True)).astype(jnp.bfloat16)
        out = jnp.einsum("hts,sd->thd", weights, value, preferred_element_type=jnp.float32)
        outs.append(out.astype(jnp.bfloat16))
    return jnp.concatenate(outs, axis=0)


def on_device(tokens, gain_attn, w_query, w_key, w_value, w_out, gain_ffn, segment_ids):
    rows_dev, width_dev = tokens.shape
    n_wa = lax.axis_size("wa")
    n_ha = lax.axis_size("ha")
    total = rows_dev * n_ha
    width = width_dev * n_wa
    head_cols = w_query.shape[1]
    heads_dev = head_cols // HD
    token_f = tokens.astype(jnp.float32)
    gain_one = gain_attn.astype(jnp.float32)
    kv_head = lax.axis_index("ha") // (n_ha // KVH)
    kv_weights = jnp.concatenate(
        [
            lax.dynamic_slice_in_dim(w_key, kv_head * HD, HD, 1),
            lax.dynamic_slice_in_dim(w_value, kv_head * HD, HD, 1),
        ],
        axis=1,
    )
    gathered = lax.all_gather(tokens, "ha", axis=0, tiled=True)
    gathered_f = gathered.astype(jnp.float32)
    row_sq = jnp.sum(gathered_f * gathered_f, axis=1)
    scaled = (gathered_f * gain_one).astype(jnp.bfloat16)
    kv_part = jnp.dot(scaled, kv_weights, preferred_element_type=jnp.float32)
    q_part = jnp.dot(scaled, w_query, preferred_element_type=jnp.float32)
    lanes = min(total, 128)
    query_f, kv_sum, sq_sum = reduce_to_ends(
        q_part, kv_part, row_sq.reshape(total // lanes, lanes), n_wa, WINDOW
    )
    row_scale = lax.rsqrt(sq_sum.reshape(total) / width + EPS)
    q_rows = total // 2
    first = jnp.where(lax.axis_index("wa") == n_wa - 1, q_rows, 0)
    kv_rows = q_rows + WINDOW

    def around(table):
        padded = jnp.pad(table, ((WINDOW, 0),) + ((0, 0),) * (table.ndim - 1))
        return lax.dynamic_slice_in_dim(padded, first, kv_rows, 0)

    index_all = jnp.arange(total, dtype=jnp.int32)
    fresh = jnp.concatenate([jnp.ones((1,), dtype=bool), segment_ids[1:] != segment_ids[:-1]])
    start_all = lax.cummax(jnp.where(fresh, index_all, jnp.zeros_like(index_all)), axis=0)
    cosine, sine = rope_tables((index_all - start_all).astype(jnp.float32))
    scale = around(row_scale)
    cosine, sine = around(cosine), around(sine)
    key_plain = (kv_sum[:, :HD] * scale[:, None]).astype(jnp.bfloat16)
    key_plain = lax.optimization_barrier(key_plain)
    value_head = (kv_sum[:, HD:] * scale[:, None]).astype(jnp.bfloat16)
    key_head = rotate(key_plain.astype(jnp.float32).reshape(kv_rows, 1, HD), cosine, sine)
    key_head = key_head.reshape(kv_rows, HD).astype(jnp.bfloat16)
    q_scale, q_cos, q_sin = scale[WINDOW:], cosine[WINDOW:], sine[WINDOW:]
    queries = rotate(
        (query_f * q_scale[:, None]).reshape(q_rows, heads_dev, HD), q_cos, q_sin
    ).astype(jnp.bfloat16)
    head_out = attend(queries, key_head, value_head, segment_ids, first)
    head_out = head_out.reshape(q_rows, head_cols)
    head_all = spread_from_ends(head_out, n_wa)
    block = head_all
    attended = lax.psum_scatter(
        jnp.dot(block, w_out, preferred_element_type=jnp.float32).astype(jnp.bfloat16),
        "ha",
        scatter_dimension=0,
        tiled=True,
    )
    residual_out = (token_f + attended.astype(jnp.float32)).astype(jnp.bfloat16)
    residual_f = residual_out.astype(jnp.float32)
    own_two = jnp.sum(residual_f * residual_f, axis=1)
    own_two = jnp.pad(own_two, (0, -rows_dev % 128)).reshape(-1, 128)
    square_two = peer_sum(own_two, n_wa).reshape(-1)[:rows_dev]
    scale_two = lax.rsqrt(square_two / width + EPS)
    ffn_input = (residual_f * scale_two[:, None] * gain_ffn.astype(jnp.float32)).astype(
        jnp.bfloat16
    )
    return (residual_out, ffn_input)


def solution(mesh):
    in_specs = (
        P("ha", "wa"),
        P("wa"),
        P("wa", "ha"),
        P("wa", None),
        P("wa", None),
        P("ha", "wa"),
        P("wa"),
        P(),
    )
    out_specs = (P("ha", "wa"), P("ha", "wa"))
    return jax.shard_map(
        on_device, mesh=mesh, in_specs=in_specs, out_specs=out_specs, check_vma=False
    )
```

profile of v0, /device:TPU:0, one launch (start us, length us, event | category | flops | bytes accessed | tf_op | source)
XLA Modules:
  0.0 424.0 jit_solution(18090039194036877210)
XLA Ops:
  7.2 0.0 all-gather.2.cloned.1.call-start
  7.2 0.7 all-gather.2.cloned.1.call-update
  7.9 0.0 reduce-scatter.2.cloned.1.call-start
  7.9 0.7 convert_element_type.72
  8.7 0.8 slice_compare_fusion
  9.5 0.1 add_select_fusion
  9.6 0.3 reduce-window.9
  9.8 0.1 slice.70
  10.0 0.8 fusion.54
  10.8 0.1 slice_reduce_fusion
  10.9 0.8 pad_dynamic-slice_fusion.5
  11.8 0.1 fusion.45
  11.9 1.9 multiply_cosine_fusion
  13.8 0.8 copy-done.1
  14.6 0.8 pad_dynamic-slice_fusion
  15.4 1.2 fusion.35
  16.6 3.0 constant_dynamic-slice_fusion
  19.6 47.3 %all-gather.2.cloned.1.call-done = bf16[1024,4096]{1,0:T(8,128)(2,1)} async-done(((bf16[128,4096]{1,0:T(8,128)(2,1)}), bf16[1024,4096]{1,0:T(8,128)(2,1)}) %all-gather.2.cloned.1.call-update) | async-done | bytes 8388624 | tf_op jit(solution)/shard_map/all_gather | solution.py:377
  66.9 5.2 %fusion.3 = f32[1024]{0:T(1024)S(1)} fusion(bf16[1024,4096]{1,0:T(8,128)(2,1)} %all-gather.2.cloned.1.call-done), kind=kLoop, calls=%fused_computation.5 | loop fusion | flops 12581888 | bytes 8392704 | tf_op jit(solution)/shard_map/reduce_sum | solution.py:379
  72.1 0.5 copy-done
  72.6 20.3 %fusion.6.q_ref = f32[1024,2048]{1,0:T(8,128)S(1)} fusion(bf16[4096,2048]{1,0:T(8,128)(2,1)} %param.10, bf16[1024,4096]{1,0:T(8,128)(2,1)S(1)} %copy-done, f32[4096]{0:T(1024)S(1)} %convert_element_type.72), kind=kOutput, calls=%fused_computation.14 | convolution fusion | flops 17192452096 | bytes 33570816 | tf_op jit(solution)/shard_map/dot_general | solution.py:382
  93.0 2.3 fusion.4.kv_ref
  95.3 129.3 %shard_map.95 = (f32[512,2048]{1,0:T(8,128)S(1)}, f32[768,256]{1,0:T(8,128)S(1)}, f32[8,128]{1,0:T(8,128)S(1)}) custom-call(f32[1024,2048]{1,0:T(8,128)S(1)} %fusion.6.q_ref, f32[1024,256]{1,0:T(8,128)S(1)} %fusion.4.kv_ref, f32[8,128]{1,0:T(8,128)S(1)} %bitcast.76), custom_call_target="tpu_custom_call" | custom-call | tf_op jit(solution)/shard_map/pallas_call | solution.py:222
  224.7 0.1 pad_dynamic-slice_fusion.6
  224.7 0.3 multiply_bitcast_fusion
  225.1 0.9 copy.33
  226.0 1.3 fusion.53
  227.4 0.2 multiply_convert_fusion.1
  227.6 0.2 subtract_convert_fusion.1
  227.9 2.7 subtract_convert_fusion
  230.6 4.6 %fusion.29 = f32[512,256,16]{1,0,2:T(8,128)} fusion(bf16[512,16,64]{2,0,1:T(8,128)(2,1)S(1)} %get-tuple-element.10, bf16[512,16,64]{2,0,1:T(8,128)(2,1)S(1)} %get-tuple-element.11, bf16[768,1,64]{2,0,1:T(8,128)(2,1)S(1)} %get-tuple-element.14, bf16[768,1,64]{2,0,1:T(8,128)(2,1)S(1)} %get-tuple-element.15), kind=kOutput, calls=%fused_computation.45 | convolution fusion | flops 539230208 | bytes 10682368 | tf_op jit(solution)/shard_map/thd,sd->hts/dot_general | solution.py:347
  235.2 1.3 fusion.31
  236.5 9.9 %fusion.56 = (f32[16,256]{1,0:T(8,128)S(1)}, f32[16,256,512]{1,2,0:T(8,128)S(1)}) fusion(f32[512,256,16]{1,0,2:T(8,128)} %fusion.29, pred[256,512]{0,1:T(8,128)(4,1)S(1)} %copy-done.9), kind=kOutput, calls=%fused_computation.103 | output fusion | flops 14680575 | bytes 16924672 | tf_op jit(solution)/shard_map/sub | solution.py:352
  246.4 6.2 %fusion.55 = (f32[16,256]{1,0:T(8,128)S(1)}, f32[16,256,512]{1,2,0:T(8,128)}) fusion(f32[512,256,16]{1,0,2:T(8,128)S(1)} %fusion.31, pred[256,512]{0,1:T(8,128)(4,1)S(1)} %copy-done.8), kind=kOutput, calls=%fused_computation.102 | output fusion | flops 14680575 | bytes 16924672 | tf_op jit(solution)/shard_map/sub | solution.py:352
  252.6 0.8 fusion.26
  253.4 2.6 copy-done.11
  256.0 0.8 fusion.27
  256.8 1.5 pad_maximum_fusion
  258.3 2.9 copy.30.x_ref
  261.3 55.7 %shard_map.96 = bf16[1024,2048]{1,0:T(8,128)(2,1)S(1)} custom-call(bf16[512,2048]{1,0:T(8,128)(2,1)S(1)} %copy.30.x_ref), custom_call_target="tpu_custom_call" | custom-call | tf_op jit(solution)/shard_map/pallas_call | solution.py:319
  317.0 21.6 %convolution_convert_fusion = bf16[1024,4096]{1,0:T(8,128)(2,1)} fusion(bf16[1024,2048]{1,0:T(8,128)(2,1)S(1)} %shard_map.96, bf16[2048,4096]{1,0:T(8,128)(2,1)} %param.13), kind=kOutput, calls=%fused_computation.12 | convolution fusion | flops 17184063488 | bytes 29360128 | tf_op jit(solution)/shard_map/dot_general | solution.py:416
  338.6 0.0 reduce-scatter.2.cloned.1.call-update
  338.6 0.7 copy-done.10
  339.3 69.3 %reduce-scatter.2.cloned.1.call-done = bf16[128,4096]{1,0:T(8,128)(2,1)} async-done(((bf16[1024,4096]{1,0:T(8,128)(2,1)}), bf16[128,4096]{1,0:T(8,128)(2,1)}) %reduce-scatter.2.cloned.1.call-update) | async-done | bytes 1048592 | tf_op jit(solution)/shard_map/reduce_scatter | solution.py:415
  408.6 1.7 fusion.18
  410.3 0.0 copy-start.3
  410.3 5.5 %shard_map.97 = f32[1,128]{1,0:T(1,128)S(1)} custom-call(f32[1,128]{1,0:T(1,128)S(1)} %bitcast.77), custom_call_target="tpu_custom_call" | custom-call | tf_op jit(solution)/shard_map/pallas_call | solution.py:86
  415.8 1.3 fusion.20
  (27 shorter events, 0.1 us)
Async XLA Ops:
  7.2 59.7 %all-gather.2.cloned.1.call-start = ((), (), s32[]{:S(2)}) async-start(), calls=%async_computation.1 | async-start | bytes 9437184 | tf_op jit(solution)/shard_map/all_gather | solution.py:377
  7.9 400.7 %reduce-scatter.2.cloned.1.call-start = ((), (), s32[]{:S(2)}) async-start(), calls=%async_computation.2 | async-start | bytes 9437184 | tf_op jit(solution)/shard_map/reduce_scatter | solution.py:415
  13.8 0.8 copy-start.1
  66.9 5.8 %copy-start = (bf16[1024,4096]{1,0:T(8,128)(2,1)S(1)}, bf16[1024,4096]{1,0:T(8,128)(2,1)}, u32[]{:S(2)}) copy-start(bf16[1024,4096]{1,0:T(8,128)(2,1)} %all-gather.2.cloned.1.call-done) | copy-start | bytes 25165828
  72.6 20.3 %copy-start.5 = (bf16[4096,128]{1,0:T(8,128)(2,1)S(1)}, bf16[4096,128]{1,0:T(8,128)(2,1)}, u32[]{:S(2)}) copy-start(bf16[4096,128]{1,0:T(8,128)(2,1)} %get-tuple-element.32) | copy-start | bytes 3145732
  72.6 20.4 %copy-start.6 = (bf16[4096,128]{1,0:T(8,128)(2,1)S(1)}, bf16[4096,128]{1,0:T(8,128)(2,1)}, u32[]{:S(2)}) copy-start(bf16[4096,128]{1,0:T(8,128)(2,1)} %get-tuple-element.33) | copy-start | bytes 3145732
  226.0 1.6 copy-start.2
  226.0 1.8 copy-start.7
  235.2 1.4 copy-start.9
  236.5 9.9 %copy-start.8 = (pred[256,512]{0,1:T(8,128)(4,1)S(1)}, pred[256,512]{0,1:T(8,128)(4,1)}, u32[]{:S(2)}) copy-start(pred[256,512]{0,1:T(8,128)(4,1)} %get-tuple-element.25) | copy-start | bytes 393220
  252.6 3.4 copy-start.11
  338.6 0.7 copy-start.10
  338.6 70.0 %copy-start.4 = (bf16[128,4096]{1,0:T(8,128)(2,1)S(1)}, bf16[128,4096]{1,0:T(8,128)(2,1)}, u32[]{:S(2)}) copy-start(bf16[128,4096]{1,0:T(8,128)(2,1)} %param.8) | copy-start | bytes 3145732
  410.3 6.8 %copy-start.3 = (bf16[128,4096]{1,0:T(8,128)(2,1)}, bf16[128,4096]{1,0:T(8,128)(2,1)S(1)}, u32[]{:S(2)}) copy-start(bf16[128,4096]{1,0:T(8,128)(2,1)S(1)} %get-tuple-element.9) | copy-start | bytes 3145732
Sparse Core Ops, SparseCore 0:
  9.9 56.9 all-gather.1
  338.7 69.8 reduce-scatter.1
where the time goes:
time: 424 us
  Pallas kernels  190 us (45%)
  waiting for transfers between devices  117 us (28%)
  matrix products  51.8 us (12%)
  other arithmetic  35.3 us (8%)
  local copies, waits for them, and re-layouts  14.8 us (3%)
  between operations  14.3 us (3%)
    pallas_call x1, Pallas kernels, reduce_to_ends(): pl.pallas_call(functools.partial(reduce_kernel, n, nc, half, window), out...  129 us
    reduce_scatter x1, waiting for transfers between devices, on_device(): lax.psum_scatter(jnp.dot(block, w_out, preferred_element_type=jnp.float32...  69.3 us
    pallas_call x1, Pallas kernels, spread_from_ends(): pl.pallas_call(functools.partial(spread_kernel, n, nc, half), out_shape=j...  55.7 us
    all_gather x1, waiting for transfers between devices, on_device(): gathered = lax.all_gather(tokens, 'ha', axis=0, tiled=True)  47.3 us
    dot_general x1, matrix products, on_device(): jnp.dot(block, w_out, preferred_element_type=jnp.float32)  21.6 us
    dot_general x1, matrix products, on_device(): q_part = jnp.dot(scaled, w_query, preferred_element_type=jnp.float32)  20.3 us
    sub x2, other arithmetic, attend(): expo = jnp.where(allowed[None], jnp.exp(scores - peak), 0.0)  16.1 us
  transfers between devices with their start and end apart: 2, of which 2 were waited for; matrix products, arithmetic and copies ran while one was open for 3% of the time, Pallas kernels for 0%

commit v1 on v0

v1 whole, which is shorter than its diff:
```python
import functools

import jax
import jax.numpy as jnp
from jax import lax
from jax.experimental import pallas as pl
from jax.experimental.pallas import tpu as pltpu
from jax.sharding import PartitionSpec as P

KVH = 8
HD = 128
WINDOW = 256
EPS = 1e-05
TILE = 256
WIDE = 512
SKEW = 2
RING = 4
F32 = jnp.float32
BF16 = jnp.bfloat16


def rope_rows():
    half = HD // 2
    inverse = 500000.0 ** (-(jnp.arange(half, dtype=F32) * 2.0 / HD))
    angle = jnp.arange(WINDOW, dtype=F32)[:, None] * inverse[None, :]
    cosine, sine = jnp.cos(angle), jnp.sin(angle)
    return jnp.concatenate([cosine, cosine, -sine, sine], axis=1)


def mirror(a, m, size):
    total, bit = 0, 1
    while bit < size:
        total = total + lax.rem(lax.div(a, bit) + lax.div(m, bit), 2) * bit
        bit *= 2
    return total


def send_to(src, dst, sems, at, **peer):
    return pltpu.make_async_remote_copy(
        src_ref=src,
        dst_ref=dst,
        send_sem=sems.at[(0,) + at],
        recv_sem=sems.at[(1,) + at],
        device_id=peer,
        device_id_type=pl.DeviceIdType.MESH,
    )


def greet(n, chips, me, chip, core):
    barrier = pltpu.get_barrier_semaphore()

    def signal(**peer):
        pl.semaphore_signal(
            barrier, inc=1, device_id=peer, device_id_type=pl.DeviceIdType.MESH
        )

    for d in range(1, n):
        signal(wa=lax.rem(me + d, n))
    for m in range(1, chips):
        signal(ha=mirror(chip, jnp.int32(m), chips) * 2 + core)
    signal(ha=chip * 2 + 1 - core)
    pl.semaphore_wait(barrier, n + chips - 1)


def column(row):
    r = row.shape[1]
    a = lax.broadcasted_iota(jnp.int32, (r, r), 0)
    b = lax.broadcasted_iota(jnp.int32, (r, r), 1)
    return jnp.sum(jnp.where(a == b, jnp.broadcast_to(row, (r, r)), 0.0), axis=1, keepdims=True)


def lane_sums(block):
    ones = jnp.ones((8, block.shape[1]), F32)
    return lax.dot_general(
        ones, block, (((1,), (1,)), ((), ())), precision=lax.Precision.HIGHEST,
        preferred_element_type=F32,
    )


def fold_lanes(x):
    total = x[:, :128]
    for g in range(1, x.shape[1] // 128):
        total = total + x[:, g * 128 : (g + 1) * 128]
    return total


def allowed_mask(seg_row, rows):
    keys = seg_row.shape[1]
    q_seg = column(seg_row[:, keys - rows :])
    q_at = lax.broadcasted_iota(jnp.int32, (rows, keys), 0) + (keys - rows)
    k_at = lax.broadcasted_iota(jnp.int32, (rows, keys), 1)
    return (q_seg == seg_row) & (k_at <= q_at)


def front_kernel(
    n, chips, rows, tiles, per_head,
    tok_hbm, gain_ref, wq_hbm, wk_hbm, wv_hbm, seg_ref, rope_ref,
    qo, kvo, sqo, cso,
    tok, scaled, w, parts, qr, ql, kr, kl, sqp, sqs, lsq,
    wsem, tsem, same_sem, pair_sem, rsem, lsem, ssem,
):
    me, ha = lax.axis_index("wa"), lax.axis_index("ha")
    core, chip = lax.rem(ha, 2), lax.div(ha, 2)
    last = n - 1
    units = tiles + 1
    count = chips * units
    hrows = rows // 2
    own_at = pl.multiple_of(core * rows, rows)
    kv_at = pl.multiple_of(lax.div(ha, per_head) * HD, HD)

    def w_copies(u):
        if u == 0:
            return [
                pltpu.make_async_copy(
                    wk_hbm.at[:, pl.ds(kv_at, HD)], w.at[0, :, pl.ds(0, HD)], wsem.at[0]
                ),
                pltpu.make_async_copy(
                    wv_hbm.at[:, pl.ds(kv_at, HD)], w.at[0, :, pl.ds(HD, HD)], wsem.at[1]
                ),
            ]
        return [
            pltpu.make_async_copy(
                wq_hbm.at[:, pl.ds((u - 1) * TILE, TILE)], w.at[u], wsem.at[u + 1]
            )
        ]

    own_copy = pltpu.make_async_copy(tok_hbm, tok.at[0, pl.ds(own_at, rows)], tsem)
    own_copy.start()
    for u in range(units):
        for copy in w_copies(u):
            copy.start()
    greet(n, chips, me, chip, core)

    def half_rows(f):
        return pl.ds(pl.multiple_of(own_at + f * hrows, hrows), hrows)

    def same_copy(m, f):
        return send_to(
            tok_hbm.at[pl.ds(f * hrows, hrows)], tok.at[m, half_rows(f)], same_sem, (m, f),
            ha=mirror(chip, m, chips) * 2 + core,
        )

    def pair_copy(m, f, first):
        src = tok_hbm.at[pl.ds(f * hrows, hrows)] if first else tok.at[m, half_rows(f)]
        return send_to(
            src, tok.at[m, half_rows(f)], pair_sem, (m, f), ha=chip * 2 + 1 - core
        )

    for f in range(2):
        pair_copy(jnp.int32(0), f, True).start()
    for m in range(1, min(3, chips)):
        for f in range(2):
            same_copy(jnp.int32(m), f).start()

    small = [
        send_to(sqs, lsq.at[d - 1], ssem, (d - 1,), wa=lax.rem(me + d, n)) for d in range(1, n)
    ]

    def prepare(m):
        there = mirror(chip, m, chips)

        @pl.loop(0, 2 * rows // 16)
        def _(g):
            at = pl.ds(pl.multiple_of(g * 16, 16), 16)
            x = tok[m, at, :].astype(F32)
            scaled[at, :] = (x * gain_ref[...].astype(F32)).astype(BF16)
            sqp[at, :] = fold_lanes(x * x)

        for e in range(2):
            sqs[pl.ds(there * 2 + e, 1), :] = lane_sums(sqp[pl.ds(e * rows, rows), :])[:1]

    def tables(m):
        for e in range(2):
            h = mirror(chip, m, chips) * 2 + e
            allowed = allowed_mask(seg_ref[h], rows)
            at = jnp.sum(jnp.where(allowed, 1.0, 0.0), axis=1, keepdims=True) - 1.0
            lanes = lax.broadcasted_iota(jnp.int32, (rows, WINDOW), 1)
            pick = jnp.where(lanes == at.astype(jnp.int32), 1.0, 0.0)
            cso[h] = jnp.dot(
                pick, rope_ref[...], precision=lax.Precision.HIGHEST,
                preferred_element_type=F32,
            )

    def handle(pos, peer, part, land, out, sems, j):
        first = send_to(part, land, sems, (j,), wa=peer)
        later = send_to(land, land, sems, (j,), wa=peer)

        @pl.when(pos == 0)
        def _():
            first.start()

        @pl.when(pos > 0)
        def _():
            later.wait_recv()

        @pl.when((pos > 0) & (pos < last))
        def _():
            land[...] = land[...] + part[...]
            later.start()

        @pl.when(pos == last)
        def _():
            out[...] = land[...] + part[...]

    def reduce_step(s, pos, peer, e, q_land, k_land, sems):
        j = s - SKEW * pos

        @pl.when((j >= 0) & (j < count))
        def _():
            m, u = lax.div(j, units), lax.rem(j, units)

            @pl.when(u == 0)
            def _():
                handle(pos, peer, parts.at[j], k_land.at[m], kvo.at[m], sems, j)

            @pl.when(u > 0)
            def _():
                jq = m * tiles + u - 1
                part = parts.at[j, pl.ds(e * rows, rows)]
                handle(pos, peer, part, q_land.at[jq], qo.at[jq], sems, j)

    right, left = jnp.minimum(me + 1, last), jnp.maximum(me - 1, 0)

    @pl.loop(0, count + SKEW * last)
    def _(s):
        m, u = lax.div(s, units), lax.rem(s, units)

        @pl.when(s < count)
        def _():
            @pl.when(u == 0)
            def _():
                @pl.when(m == 0)
                def _():
                    own_copy.wait()

                for f in range(2):
                    pair_copy(m, f, False).wait_recv()
                prepare(m)

                @pl.when(m == chips - 1)
                def _():
                    for copy in small:
                        copy.start()

            for v in range(units):

                @pl.when(s == v)
                def _():
                    for copy in w_copies(v):
                        copy.wait()

            parts[s] = jnp.dot(scaled[...], w[u], preferred_element_type=F32)

        reduce_step(s, me, right, 1, qr, kr, rsem)
        reduce_step(s, last - me, left, 0, ql, kl, lsem)

        @pl.when((s < count) & (u == 1))
        def _():
            tables(m)

        for f in range(2):
            turn = max(0, units - 4) if f == 0 else units - 1

            @pl.when((u == turn) & (m + 1 < chips))
            def _():
                same_copy(m + 1, f).wait_recv()
                pair_copy(m + 1, f, False).start()

            @pl.when((u == turn) & (m + 3 < chips))
            def _():
                same_copy(m + 3, f).start()

    def drain(j, pos, peer, e, q_land, k_land, sems):
        m, u = lax.div(j, units), lax.rem(j, units)

        @pl.when((pos < last) & (u == 0))
        def _():
            send_to(k_land.at[m], k_land.at[m], sems, (j,), wa=peer).wait_send()

        @pl.when((pos < last) & (u > 0))
        def _():
            jq = m * tiles + u - 1
            send_to(q_land.at[jq], q_land.at[jq], sems, (j,), wa=peer).wait_send()

    @pl.loop(0, count)
    def _(j):
        drain(j, me, right, 1, qr, kr, rsem)
        drain(j, last - me, left, 0, ql, kl, lsem)

    for m in range(chips):
        for f in range(2):
            pair_copy(jnp.int32(m), f, False).wait_send()
            if m:
                same_copy(jnp.int32(m), f).wait_send()
    for copy in small:
        copy.wait()
    total = sqs[...]
    for d in range(n - 1):
        total = total + lsq[d]
    sqo[...] = total


def front(tokens, gain, w_query, w_key, w_value, seg_rows, rope, n, n_ha):
    rows, width = tokens.shape
    cols = w_query.shape[1]
    chips, tiles = n_ha // 2, cols // TILE
    units = tiles + 1
    count = chips * units
    vmem, any_ = pl.BlockSpec(memory_space=pltpu.VMEM), pl.BlockSpec(memory_space=pl.ANY)
    dma = pltpu.SemaphoreType.DMA
    return pl.pallas_call(
        functools.partial(front_kernel, n, chips, rows, tiles, n_ha // KVH),
        out_shape=(
            jax.ShapeDtypeStruct((chips * tiles, rows, TILE), F32),
            jax.ShapeDtypeStruct((chips, 2 * rows, TILE), F32),
            jax.ShapeDtypeStruct((n_ha, rows), F32),
            jax.ShapeDtypeStruct((n_ha, rows, 2 * HD), F32),
        ),
        in_specs=[any_, vmem, any_, any_, any_, vmem, vmem],
        out_specs=(vmem,) * 4,
        scratch_shapes=[
            pltpu.VMEM((chips, 2 * rows, width), BF16),
            pltpu.VMEM((2 * rows, width), BF16),
            pltpu.VMEM((units, width, TILE), BF16),
            pltpu.VMEM((count, 2 * rows, TILE), F32),
            pltpu.VMEM((chips * tiles, rows, TILE), F32),
            pltpu.VMEM((chips * tiles, rows, TILE), F32),
            pltpu.VMEM((chips, 2 * rows, TILE), F32),
            pltpu.VMEM((chips, 2 * rows, TILE), F32),
            pltpu.VMEM((2 * rows, 128), F32),
            pltpu.VMEM((n_ha, rows), F32),
            pltpu.VMEM((n - 1, n_ha, rows), F32),
            dma((units + 1,)),
            dma,
            dma((2, chips, 2)),
            dma((2, chips, 2)),
            dma((2, count)),
            dma((2, count)),
            dma((2, n - 1)),
        ],
        compiler_params=pltpu.CompilerParams(
            collective_id=0, has_side_effects=True, vmem_limit_bytes=60 << 20
        ),
    )(tokens, gain, w_query, w_key, w_value, seg_rows, rope)


def back_kernel(
    n, chips, rows, tiles, wides, all_width,
    q_ref, kv_ref, sq_ref, cs_ref, seg_ref, tok_ref, gain_ref, wo_hbm,
    res_ref, ffn_ref,
    wo, keys, values, mask, head, acc, got, stage, land, own, sqp, sq2, lsq2,
    wsem, rsem, lsem, psem, xsem, ssem,
):
    me, ha = lax.axis_index("wa"), lax.axis_index("ha")
    core, chip = lax.rem(ha, 2), lax.div(ha, 2)
    last = n - 1
    n_chunk, n_unit = chips * tiles, chips * wides
    lag = tiles + SKEW * last
    window = WINDOW + rows
    end_row = jnp.where(me == last, 1, 0)
    partner = chip * 2 + 1 - core
    mine = pl.ds(pl.multiple_of(core * rows, rows), rows)
    theirs = pl.ds(pl.multiple_of((1 - core) * rows, rows), rows)

    def w_copy(k):
        return pltpu.make_async_copy(wo_hbm.at[:, pl.ds(k * WIDE, WIDE)], wo.at[k], wsem.at[k])

    for k in range(wides):
        w_copy(k).start()
    greet(n, chips, me, chip, core)

    def row_scale(h):
        return column(lax.rsqrt(sq_ref[pl.ds(h, 1), :] / all_width + EPS))

    def rotated(x, h):
        return x * cs_ref[h, :, :HD] + pltpu.roll(x, HD // 2, 1) * cs_ref[h, :, HD:]

    is_end = (me == 0) | (me == last)

    @pl.when(is_end)
    def _():
        zero = jnp.zeros((WINDOW, HD), BF16)
        keys[pl.ds(0, WINDOW), :] = zero
        values[pl.ds(0, WINDOW), :] = zero

        @pl.loop(0, chips)
        def _(m):
            there = mirror(chip, m, chips)
            for e in range(2):
                h = there * 2 + e
                at = pl.ds(pl.multiple_of(WINDOW + h * rows, rows), rows)
                scale = row_scale(h)
                block = kv_ref.at[m, pl.ds(e * rows, rows)]
                plain = (block[:, :HD] * scale).astype(BF16).astype(F32)
                keys[at, :] = rotated(plain, h).astype(BF16)
                values[at, :] = (block[:, HD:] * scale).astype(BF16)

    def attend(j):
        p, t = lax.div(j, tiles), lax.rem(j, tiles)
        m = chips - 1 - p
        h = mirror(chip, m, chips) * 2 + end_row

        @pl.when(t == 0)
        def _():
            mask[...] = jnp.where(allowed_mask(seg_ref[h], rows), 1.0, 0.0)

        at = pl.ds(pl.multiple_of(h * rows, rows), window)
        scale = row_scale(h)
        allowed = mask[...] > 0.5
        to = pl.ds(pl.multiple_of(end_row * rows, rows), rows)
        for x in range(TILE // HD):
            query = rotated(q_ref[m * tiles + t, :, x * HD : (x + 1) * HD] * scale, h).astype(BF16)
            scores = lax.dot_general(
                query, keys[at, :], (((1,), (1,)), ((), ())), preferred_element_type=F32
            ) * HD ** (-0.5)
            scores = jnp.where(allowed, scores, -1e30)
            peak = jnp.max(scores, axis=1, keepdims=True)
            expo = jnp.where(allowed, jnp.exp(scores - peak), 0.0)
            weights = (expo / jnp.sum(expo, axis=1, keepdims=True)).astype(BF16)
            out = jnp.dot(weights, values[at, :], preferred_element_type=F32)
            head[p, t, to, x * HD : (x + 1) * HD] = out.astype(BF16)

    def spread_copy(j, e, peer, sems):
        ref = head.at[lax.div(j, tiles), lax.rem(j, tiles), pl.ds(e * rows, rows)]
        return send_to(ref, ref, sems, (j,), wa=peer)

    def spread_step(s, pos, peer, e, sems):
        j = s - SKEW * pos

        @pl.when((j >= 0) & (j < n_chunk))
        def _():
            copy = spread_copy(j, e, peer, sems)

            @pl.when(pos > 0)
            def _():
                copy.wait_recv()

            @pl.when(pos < last)
            def _():
                copy.start()

    def pair_copy(v):
        return send_to(acc.at[lax.rem(v, RING), theirs], got.at[v], psem, (v,), ha=partner)

    def peer_copy(v):
        m = chips - 1 - lax.div(v, wides)
        return send_to(
            stage.at[v], land.at[v], xsem, (v,), ha=mirror(chip, m, chips) * 2 + core
        )

    def project(v):
        p, k = lax.div(v, wides), lax.rem(v, wides)
        for i in range(wides):

            @pl.when(v == i)
            def _():
                w_copy(i).wait()

        @pl.when(v >= RING)
        def _():
            pair_copy(v - RING).wait_send()

        block = jnp.concatenate([head[p, t] for t in range(tiles)], axis=1)
        for y in range(WIDE // TILE):
            at = slice(y * TILE, (y + 1) * TILE)
            acc[lax.rem(v, RING), :, at] = jnp.dot(
                block, wo[k, :, at], preferred_element_type=F32
            )
        pair_copy(v).start()

    def combine(v):
        p, k = lax.div(v, wides), lax.rem(v, wides)
        pair_copy(v).wait_recv()
        both = acc[lax.rem(v, RING), mine, :] + got[v]

        @pl.when(p < chips - 1)
        def _():
            stage[v] = both.astype(BF16)
            peer_copy(v).start()

        @pl.when(p == chips - 1)
        def _():
            own[k] = both

    right, left = jnp.minimum(me + 1, last), jnp.maximum(me - 1, 0)

    @pl.loop(0, n_unit + lag + 1)
    def _(s):
        @pl.when(is_end & (s < n_chunk))
        def _():
            attend(s)

        spread_step(s, me, right, 0, rsem)
        spread_step(s, last - me, left, 1, lsem)

        v = s - lag

        @pl.when((v >= 0) & (v < n_unit))
        def _():
            project(v)

        @pl.when(v >= 1)
        def _():
            combine(v - 1)

    @pl.loop(0, wides)
    def _(k):
        total = own[k]
        for p in range(chips - 1):
            peer_copy(p * wides + k).wait_recv()
            total = total + land[p * wides + k].astype(F32)
        at = pl.ds(pl.multiple_of(k * WIDE, WIDE), WIDE)
        res = (tok_ref[:, at].astype(F32) + total).astype(BF16)
        res_ref[:, at] = res
        wide = res.astype(F32)
        square = fold_lanes(wide * wide)

        @pl.when(k == 0)
        def _():
            sqp[...] = square

        @pl.when(k > 0)
        def _():
            sqp[...] = sqp[...] + square

    sq2[...] = lane_sums(sqp[...])
    small = [
        send_to(sq2, lsq2.at[d - 1], ssem, (d - 1,), wa=lax.rem(me + d, n)) for d in range(1, n)
    ]
    for copy in small:
        copy.start()

    @pl.loop(0, n_chunk)
    def _(j):
        @pl.when(me < last)
        def _():
            spread_copy(j, 0, right, rsem).wait_send()

        @pl.when(me > 0)
        def _():
            spread_copy(j, 1, left, lsem).wait_send()

    @pl.loop(0, n_unit - wides)
    def _(v):
        peer_copy(v).wait_send()

    for v in range(n_unit - RING, n_unit):
        pair_copy(jnp.int32(v)).wait_send()
    for copy in small:
        copy.wait()
    total = sq2[...]
    for d in range(n - 1):
        total = total + lsq2[d]
    scale_two = column(lax.rsqrt(total[:1] / all_width + EPS))

    @pl.loop(0, wides)
    def _(k):
        at = pl.ds(pl.multiple_of(k * WIDE, WIDE), WIDE)
        wide = res_ref[:, at].astype(F32)
        ffn_ref[:, at] = (wide * scale_two * gain_ref[:, at].astype(F32)).astype(BF16)


def back(q_sum, kv_sum, sq_sum, cs, seg_rows, tokens, gain, w_out, n, n_ha):
    rows, width = tokens.shape
    cols = w_out.shape[0]
    chips, tiles, wides = n_ha // 2, cols // TILE, width // WIDE
    n_chunk, n_unit = chips * tiles, chips * wides
    vmem, any_ = pl.BlockSpec(memory_space=pltpu.VMEM), pl.BlockSpec(memory_space=pl.ANY)
    dma = pltpu.SemaphoreType.DMA
    out = jax.ShapeDtypeStruct((rows, width), BF16)
    return pl.pallas_call(
        functools.partial(back_kernel, n, chips, rows, tiles, wides, width * n),
        out_shape=(out, out),
        in_specs=[vmem] * 7 + [any_],
        out_specs=(vmem, vmem),
        scratch_shapes=[
            pltpu.VMEM((wides, cols, WIDE), BF16),
            pltpu.VMEM((WINDOW + n_ha * rows, HD), BF16),
            pltpu.VMEM((WINDOW + n_ha * rows, HD), BF16),
            pltpu.VMEM((rows, WINDOW + rows), F32),
            pltpu.VMEM((chips, tiles, 2 * rows, TILE), BF16),
            pltpu.VMEM((RING, 2 * rows, WIDE), F32),
            pltpu.VMEM((n_unit, rows, WIDE), F32),
            pltpu.VMEM((n_unit - wides, rows, WIDE), BF16),
            pltpu.VMEM((n_unit - wides, rows, WIDE), BF16),
            pltpu.VMEM((wides, rows, WIDE), F32),
            pltpu.VMEM((rows, 128), F32),
            pltpu.VMEM((8, rows), F32),
            pltpu.VMEM((n - 1, 8, rows), F32),
            dma((wides,)),
            dma((2, n_chunk)),
            dma((2, n_chunk)),
            dma((2, n_unit)),
            dma((2, n_unit - wides)),
            dma((2, n - 1)),
        ],
        compiler_params=pltpu.CompilerParams(
            collective_id=1, has_side_effects=True, vmem_limit_bytes=60 << 20
        ),
    )(q_sum, kv_sum, sq_sum, cs, seg_rows, tokens, gain, w_out)


def on_device(tokens, gain_attn, w_query, w_key, w_value, w_out, gain_ffn, segment_ids):
    rows, width = tokens.shape
    n_wa = lax.axis_size("wa")
    n_ha = lax.axis_size("ha")
    padded = jnp.pad(segment_ids, (WINDOW, 0), constant_values=-1).astype(F32)
    seg_rows = jnp.stack([padded[None, h * rows : (h + 1) * rows + WINDOW] for h in range(n_ha)])
    q_sum, kv_sum, sq_sum, cs = front(
        tokens, gain_attn.reshape(1, width), w_query, w_key, w_value, seg_rows, rope_rows(),
        n_wa, n_ha,
    )
    return back(
        q_sum, kv_sum, sq_sum, cs, seg_rows, tokens, gain_ffn.reshape(1, width), w_out,
        n_wa, n_ha,
    )


def solution(mesh):
    in_specs = (
        P("ha", "wa"),
        P("wa"),
        P("wa", "ha"),
        P("wa", None),
        P("wa", None),
        P("ha", "wa"),
        P("wa"),
        P(),
    )
    out_specs = (P("ha", "wa"), P("ha", "wa"))
    return jax.shard_map(
        on_device, mesh=mesh, in_specs=in_specs, out_specs=out_specs, check_vma=False
    )
```

time: 424 us -> 259 us (0.61)
  waiting for transfers between devices: 117 us -> 0 us
  Pallas kernels: 190 us -> 249 us
  matrix products: 51.8 us -> 0 us
  other arithmetic: 35.3 us -> 2.09 us
  between operations: 14.3 us -> 0.69 us
  local copies, waits for them, and re-layouts: 14.8 us -> 7.27 us
    reduce_scatter x1 -> x0, waiting for transfers between devices: 69.3 us -> none  [on_device(): lax.psum_scatter(jnp.dot(block, w_out, preferred_element_type=jnp.float32...]
    pallas_call x3 -> x2, Pallas kernels: 190 us -> 249 us  [the longest x1 153 us: front(): pl.pallas_call(functools.partial(front_kernel, n, chips, rows, tiles, n_h...]
    dot_general x7 -> x0, matrix products: 51.8 us -> none  [the longest x1 21.6 us: on_device(): jnp.dot(block, w_out, preferred_element_type=jnp.float32)]
    all_gather x1 -> x0, waiting for transfers between devices: 47.3 us -> none  [on_device(): gathered = lax.all_gather(tokens, 'ha', axis=0, tiled=True)]
    sub x2 -> x0, other arithmetic: 16.1 us -> none  [attend(): expo = jnp.where(allowed[None], jnp.exp(scores - peak), 0.0)]
    reduce_sum x2 -> x0, other arithmetic: 6.9 us -> none  [the longest x1 5.22 us: on_device(): row_sq = jnp.sum(gathered_f * gathered_f, axis=1)]
  transfers between devices with their start and end apart: 2 -> 0, of which waited for: 2 -> 0; matrix products, arithmetic and copies ran while one was open for 3% -> 0% of each run, Pallas kernels for 0% -> 0%
where the time goes in v1:
time: 259 us
  Pallas kernels  249 us (96%)
  local copies, waits for them, and re-layouts  7.27 us (3%)
    pallas_call x1, Pallas kernels, front(): pl.pallas_call(functools.partial(front_kernel, n, chips, rows, tiles, n_h...  153 us
    pallas_call x1, Pallas kernels, back(): pl.pallas_call(functools.partial(back_kernel, n, chips, rows, tiles, wide...  95.5 us

profile of v1, /device:TPU:0, one launch (start us, length us, event | category | flops | bytes accessed | tf_op | source)
XLA Modules:
  0.0 258.8 jit_solution(11135557727354156289)
XLA Ops:
  0.6 0.7 pad_convert_fusion
  1.4 0.0 copy-start
  1.4 1.3 reshape.16.gain_ref
  2.8 1.3 reshape.17.gain_ref
  4.1 0.5 fusion.1
  4.6 0.9 pad_maximum_fusion.rope_ref
  5.5 0.0 copy-done
  5.5 153.3 %shard_map.95 = (f32[32,128,256]{2,1,0:T(8,128)}, f32[4,256,256]{2,1,0:T(8,128)}, f32[8,128]{1,0:T(8,128)}, f32[8,128,256]{2,1,0:T(8,128)}) custom-call(bf16[128,4096]{1,0:T(8,128)(2,1)} %tok_ref.1, bf16[1,4096]{1,0:T(2,128)(2,1)} %reshape.16.gain_ref, bf16[4096,2048]{1,0:T(8,128)(2,1)} %wq_hbm.1, bf16[4096,1024]{1,0:T(8,128)(2,1)} %wk_hbm.1, ...), custom_call_target="tpu_custom_call" | custom-call | tf_op jit(solution)/shard_map/pallas_call | solution.py:311
  158.8 95.5 %shard_map.96 = (bf16[128,4096]{1,0:T(8,128)(2,1)}, bf16[128,4096]{1,0:T(8,128)(2,1)}) custom-call(f32[32,128,256]{2,1,0:T(8,128)} %get-tuple-element.6.q_ref, f32[4,256,256]{2,1,0:T(8,128)} %get-tuple-element.7.kv_ref, f32[8,128]{1,0:T(8,128)} %get-tuple-element.8.sq_ref, f32[8,128,256]{2,1,0:T(8,128)} %get-tuple-element.9.cs_ref, f32[8,1,384]{2,1,0:T(1,128)} %copy-done, ...), custom_call_target="tpu_custom_call" | custom-call | tf_op jit(solution)/shard_map/pallas_call | solution.py:571
  254.2 2.3 copy.19
  256.5 2.3 copy.20
  (10 shorter events, 0.1 us)
Async XLA Ops:
  1.4 4.0 %copy-start = (f32[8,1,384]{2,1,0:T(1,128)}, f32[8,1,384]{2,1,0:T(1,128)S(1)}, u32[]{:S(2)}) copy-start(f32[8,1,384]{2,1,0:T(1,128)S(1)} %constant_dynamic-update-slice_fusion.seg_ref) | copy-start | bytes 36868

commit v2 on v1

--- a/solution.py
+++ b/solution.py
@@ -13,7 +13,9 @@
 EPS = 1e-05
 TILE = 256
 WIDE = 512
-SKEW = 2
+SKEW = 3
+LEVELS = 32766.0
+FORWARD = 2
 RING = 4
 F32 = jnp.float32
 BF16 = jnp.bfloat16
@@ -33,6 +35,18 @@
         total = total + lax.rem(lax.div(a, bit) + lax.div(m, bit), 2) * bit
         bit *= 2
     return total
+
+
+def member(g, sub, chips):
+    edge = (g == 0) | (g == chips - 1)
+    low = lax.div(g - 1, 2) * 2 + 1
+    return jnp.where(edge, g, low + sub), jnp.where(edge, sub, lax.rem(g - 1, 2))
+
+
+def place(m, f, chips):
+    edge = (m == 0) | (m == chips - 1)
+    low = lax.div(m - 1, 2) * 2 + 1
+    return jnp.where(edge, m, low + f), jnp.where(edge, f, lax.rem(m - 1, 2))
 
 
 def send_to(src, dst, sems, at, **peer):
@@ -69,6 +83,36 @@
     return jnp.sum(jnp.where(a == b, jnp.broadcast_to(row, (r, r)), 0.0), axis=1, keepdims=True)
 
 
+def as_row(col):
+    r = col.shape[0]
+    a = lax.broadcasted_iota(jnp.int32, (r, r), 0)
+    b = lax.broadcasted_iota(jnp.int32, (r, r), 1)
+    return jnp.sum(jnp.where(a == b, jnp.broadcast_to(col, (r, r)), 0.0), axis=0, keepdims=True)
+
+
+def encode(x, code, steps, rows):
+    for i in range(x.shape[0] // rows):
+        for y in range(TILE // HD):
+            part = x[i * rows : (i + 1) * rows, y * HD : (y + 1) * HD]
+            top = jnp.maximum(jnp.max(jnp.abs(part), axis=1, keepdims=True), 1e-30)
+            whole = jnp.round(part * (LEVELS / top)).astype(jnp.int32)
+            code[i * rows : (i + 1) * rows, y * HD : (y + 1) * HD] = whole.astype(jnp.int16)
+            k = i * 2 + y
+            steps[k : k + 1, :] = as_row(top * (1.0 / LEVELS))
+
+
+def decode(code, steps, rows):
+    blocks = []
+    for i in range(code.shape[0] // rows):
+        line = []
+        for y in range(TILE // HD):
+            part = code[i * rows : (i + 1) * rows, y * HD : (y + 1) * HD]
+            k = i * 2 + y
+            line.append(part.astype(jnp.int32).astype(F32) * column(steps[k : k + 1, :]))
+        blocks.append(jnp.concatenate(line, axis=1))
+    return jnp.concatenate(blocks, axis=0)
+
+
 def lane_sums(block):
     ones = jnp.ones((8, block.shape[1]), F32)
     return lax.dot_general(
@@ -96,8 +140,8 @@
     n, chips, rows, tiles, per_head,
     tok_hbm, gain_ref, wq_hbm, wk_hbm, wv_hbm, seg_ref, rope_ref,
     qo, kvo, sqo, cso,
-    tok, scaled, w, parts, qr, ql, kr, kl, sqp, sqs, lsq,
-    wsem, tsem, same_sem, pair_sem, rsem, lsem, ssem,
+    tok, scaled, w, parts, qr, ql, kr, kl, er, el, sqp, sqs, lsq,
+    wsem, tsem, same_sem, pair_sem, rsem, lsem, resem, lesem, ssem,
 ):
     me, ha = lax.axis_index("wa"), lax.axis_index("ha")
     core, chip = lax.rem(ha, 2), lax.div(ha, 2)
@@ -132,77 +176,88 @@
     greet(n, chips, me, chip, core)
 
     def half_rows(f):
-        return pl.ds(pl.multiple_of(own_at + f * hrows, hrows), hrows)
+        return pl.ds(pl.multiple_of(f * hrows, hrows), hrows)
+
+    def spot(m, f):
+        g, part = place(m, f, chips)
+        return tok.at[g, pl.ds(pl.multiple_of(own_at + part * hrows, hrows), hrows)]
 
     def same_copy(m, f):
         return send_to(
-            tok_hbm.at[pl.ds(f * hrows, hrows)], tok.at[m, half_rows(f)], same_sem, (m, f),
+            tok_hbm.at[half_rows(f)], spot(m, f), same_sem, (m, f),
             ha=mirror(chip, m, chips) * 2 + core,
         )
 
     def pair_copy(m, f, first):
-        src = tok_hbm.at[pl.ds(f * hrows, hrows)] if first else tok.at[m, half_rows(f)]
-        return send_to(
-            src, tok.at[m, half_rows(f)], pair_sem, (m, f), ha=chip * 2 + 1 - core
-        )
+        src = tok_hbm.at[half_rows(f)] if first else spot(m, f)
+        return send_to(src, spot(m, f), pair_sem, (m, f), ha=chip * 2 + 1 - core)
 
     for f in range(2):
         pair_copy(jnp.int32(0), f, True).start()
-    for m in range(1, min(3, chips)):
-        for f in range(2):
+    for f in range(2):
+        for m in range(1, min(3, chips)):
             same_copy(jnp.int32(m), f).start()
 
     small = [
         send_to(sqs, lsq.at[d - 1], ssem, (d - 1,), wa=lax.rem(me + d, n)) for d in range(1, n)
     ]
 
-    def prepare(m):
-        there = mirror(chip, m, chips)
-
+    def prepare(g):
         @pl.loop(0, 2 * rows // 16)
-        def _(g):
-            at = pl.ds(pl.multiple_of(g * 16, 16), 16)
-            x = tok[m, at, :].astype(F32)
+        def _(i):
+            at = pl.ds(pl.multiple_of(i * 16, 16), 16)
+            x = tok[g, at, :].astype(F32)
             scaled[at, :] = (x * gain_ref[...].astype(F32)).astype(BF16)
             sqp[at, :] = fold_lanes(x * x)
 
         for e in range(2):
-            sqs[pl.ds(there * 2 + e, 1), :] = lane_sums(sqp[pl.ds(e * rows, rows), :])[:1]
-
-    def tables(m):
+            sqs[pl.ds(g * 2 + e, 1), :] = lane_sums(sqp[pl.ds(e * rows, rows), :])[:1]
+
+    def tables(g):
         for e in range(2):
-            h = mirror(chip, m, chips) * 2 + e
-            allowed = allowed_mask(seg_ref[h], rows)
-            at = jnp.sum(jnp.where(allowed, 1.0, 0.0), axis=1, keepdims=True) - 1.0
-            lanes = lax.broadcasted_iota(jnp.int32, (rows, WINDOW), 1)
-            pick = jnp.where(lanes == at.astype(jnp.int32), 1.0, 0.0)
-            cso[h] = jnp.dot(
-                pick, rope_ref[...], precision=lax.Precision.HIGHEST,
-                preferred_element_type=F32,
-            )
-
-    def handle(pos, peer, part, land, out, sems, j):
-        first = send_to(part, land, sems, (j,), wa=peer)
-        later = send_to(land, land, sems, (j,), wa=peer)
+            for part in range(2):
+                m, f = member(g, part, chips)
+                allowed = allowed_mask(seg_ref[(mirror(chip, m, chips) * 2 + e) * 2 + f], hrows)
+                at = jnp.sum(jnp.where(allowed, 1.0, 0.0), axis=1, keepdims=True) - 1.0
+                lanes = lax.broadcasted_iota(jnp.int32, (hrows, WINDOW), 1)
+                pick = jnp.where(lanes == at.astype(jnp.int32), 1.0, 0.0)
+                cso[g * 2 + e, part * hrows : (part + 1) * hrows, :] = jnp.dot(
+                    pick, rope_ref[...], precision=lax.Precision.HIGHEST,
+                    preferred_element_type=F32,
+                )
+
+    def code_copies(land, steps, sems, step_sems, j, peer):
+        return (
+            send_to(land, land, sems, (j,), wa=peer),
+            send_to(steps, steps, step_sems, (j,), wa=peer),
+        )
+
+    def handle(pos, peer, part, land, steps, out, sems, step_sems, j):
+        copies = code_copies(land, steps, sems, step_sems, j, peer)
 
         @pl.when(pos == 0)
         def _():
-            first.start()
+            encode(part[...], land, steps, rows)
 
         @pl.when(pos > 0)
         def _():
-            later.wait_recv()
+            for copy in copies:
+                copy.wait_recv()
 
         @pl.when((pos > 0) & (pos < last))
         def _():
-            land[...] = land[...] + part[...]
-            later.start()
+            encode(decode(land, steps, rows) + part[...], land, steps, rows)
+
+        @pl.when(pos < last)
+        def _():
+            for copy in copies:
+                copy.start()
 
         @pl.when(pos == last)
         def _():
-            out[...] = land[...] + part[...]
-
-    def reduce_step(s, pos, peer, e, q_land, k_land, sems):
+            out[...] = decode(land, steps, rows) + part[...]
+
+    def reduce_step(s, pos, peer, e, q_land, k_land, steps, sems, step_sems):
         j = s - SKEW * pos
 
         @pl.when((j >= 0) & (j < count))
@@ -211,33 +266,39 @@
 
             @pl.when(u == 0)
             def _():
-                handle(pos, peer, parts.at[j], k_land.at[m], kvo.at[m], sems, j)
+                handle(
+                    pos, peer, parts.at[j], k_land.at[m], steps.at[j], kvo.at[m],
+                    sems, step_sems, j,
+                )
 
             @pl.when(u > 0)
             def _():
                 jq = m * tiles + u - 1
                 part = parts.at[j, pl.ds(e * rows, rows)]
-                handle(pos, peer, part, q_land.at[jq], qo.at[jq], sems, j)
+                handle(
+                    pos, peer, part, q_land.at[jq], steps.at[j], qo.at[jq],
+                    sems, step_sems, j,
+                )
 
     right, left = jnp.minimum(me + 1, last), jnp.maximum(me - 1, 0)
 
     @pl.loop(0, count + SKEW * last)
     def _(s):
-        m, u = lax.div(s, units), lax.rem(s, units)
+        g, u = lax.div(s, units), lax.rem(s, units)
 
         @pl.when(s < count)
         def _():
             @pl.when(u == 0)
             def _():
-                @pl.when(m == 0)
+                @pl.when(g == 0)
                 def _():
                     own_copy.wait()
 
-                for f in range(2):
-                    pair_copy(m, f, False).wait_recv()
-                prepare(m)
-
-                @pl.when(m == chips - 1)
+                for part in range(2):
+                    pair_copy(*member(g, part, chips), False).wait_recv()
+                prepare(g)
+
+                @pl.when(g == chips - 1)
                 def _():
                     for copy in small:
                         copy.start()
@@ -251,41 +312,43 @@
 
             parts[s] = jnp.dot(scaled[...], w[u], preferred_element_type=F32)
 
-        reduce_step(s, me, right, 1, qr, kr, rsem)
-        reduce_step(s, last - me, left, 0, ql, kl, lsem)
+        reduce_step(s, me, right, 1, qr, kr, er, rsem, resem)
+        reduce_step(s, last - me, left, 0, ql, kl, el, lsem, lesem)
 
         @pl.when((s < count) & (u == 1))
         def _():
-            tables(m)
-
-        for f in range(2):
-            turn = max(0, units - 4) if f == 0 else units - 1
-
-            @pl.when((u == turn) & (m + 1 < chips))
+            tables(g)
+
+        @pl.when((u == max(0, units - FORWARD)) & (g + 1 < chips))
+        def _():
+            @pl.when(g + 3 < chips)
             def _():
-                same_copy(m + 1, f).wait_recv()
-                pair_copy(m + 1, f, False).start()
-
-            @pl.when((u == turn) & (m + 3 < chips))
-            def _():
-                same_copy(m + 3, f).start()
-
-    def drain(j, pos, peer, e, q_land, k_land, sems):
+                for f in range(2):
+                    same_copy(g + 3, f).start()
+
+            for part in range(2):
+                m, f = member(g + 1, part, chips)
+                same_copy(m, f).wait_recv()
+                pair_copy(m, f, False).start()
+
+    def drain(j, pos, peer, q_land, k_land, steps, sems, step_sems):
         m, u = lax.div(j, units), lax.rem(j, units)
 
         @pl.when((pos < last) & (u == 0))
         def _():
-            send_to(k_land.at[m], k_land.at[m], sems, (j,), wa=peer).wait_send()
+            for copy in code_copies(k_land.at[m], steps.at[j], sems, step_sems, j, peer):
+                copy.wait_send()
 
         @pl.when((pos < last) & (u > 0))
         def _():
             jq = m * tiles + u - 1
-            send_to(q_land.at[jq], q_land.at[jq], sems, (j,), wa=peer).wait_send()
+            for copy in code_copies(q_land.at[jq], steps.at[j], sems, step_sems, j, peer):
+                copy.wait_send()
 
     @pl.loop(0, count)
     def _(j):
-        drain(j, me, right, 1, qr, kr, rsem)
-        drain(j, last - me, left, 0, ql, kl, lsem)
+        drain(j, me, right, qr, kr, er, rsem, resem)
+        drain(j, last - me, left, ql, kl, el, lsem, lesem)
 
     for m in range(chips):
         for f in range(2):
@@ -323,10 +386,12 @@
             pltpu.VMEM((2 * rows, width), BF16),
             pltpu.VMEM((units, width, TILE), BF16),
             pltpu.VMEM((count, 2 * rows, TILE), F32),
-            pltpu.VMEM((chips * tiles, rows, TILE), F32),
-            pltpu.VMEM((chips * tiles, rows, TILE), F32),
-            pltpu.VMEM((chips, 2 * rows, TILE), F32),
-            pltpu.VMEM((chips, 2 * rows, TILE), F32),
+            pltpu.VMEM((chips * tiles, rows, TILE), jnp.int16),
+            pltpu.VMEM((chips * tiles, rows, TILE), jnp.int16),
+            pltpu.VMEM((chips, 2 * rows, TILE), jnp.int16),
+            pltpu.VMEM((chips, 2 * rows, TILE), jnp.int16),
+            pltpu.VMEM((count, 8, rows), F32),
+            pltpu.VMEM((count, 8, rows), F32),
             pltpu.VMEM((2 * rows, 128), F32),
             pltpu.VMEM((n_ha, rows), F32),
             pltpu.VMEM((n - 1, n_ha, rows), F32),
@@ -336,6 +401,8 @@
             dma((2, chips, 2)),
             dma((2, count)),
             dma((2, count)),
+            dma((2, count)),
+            dma((2, count)),
             dma((2, n - 1)),
         ],
         compiler_params=pltpu.CompilerParams(
@@ -346,9 +413,9 @@
 
 def back_kernel(
     n, chips, rows, tiles, wides, all_width,
-    q_ref, kv_ref, sq_ref, cs_ref, seg_ref, tok_ref, gain_ref, wo_hbm,
-    res_ref, ffn_ref,
-    wo, keys, values, mask, head, acc, got, stage, land, own, sqp, sq2, lsq2,
+    q_ref, kv_ref, sq_ref, cs_ref, seg_ref, tok_ref, wo_hbm,
+    sum_ref, sqo_ref,
+    wo, keys, values, mask, qscale, head, acc, got, stage, land, own, sqp, sq2, lsq2,
     wsem, rsem, lsem, psem, xsem, ssem,
 ):
     me, ha = lax.axis_index("wa"), lax.axis_index("ha")
@@ -356,7 +423,8 @@
     last = n - 1
     n_chunk, n_unit = chips * tiles, chips * wides
     lag = tiles + SKEW * last
-    window = WINDOW + rows
+    hrows = rows // 2
+    window = WINDOW + hrows
     end_row = jnp.where(me == last, 1, 0)
     partner = chip * 2 + 1 - core
     mine = pl.ds(pl.multiple_of(core * rows, rows), rows)
@@ -369,11 +437,16 @@
         w_copy(k).start()
     greet(n, chips, me, chip, core)
 
-    def row_scale(h):
-        return column(lax.rsqrt(sq_ref[pl.ds(h, 1), :] / all_width + EPS))
-
-    def rotated(x, h):
-        return x * cs_ref[h, :, :HD] + pltpu.roll(x, HD // 2, 1) * cs_ref[h, :, HD:]
+    def row_scale(k):
+        return column(lax.rsqrt(sq_ref[pl.ds(k, 1), :] / all_width + EPS))
+
+    def rotated(x, cs):
+        return x * cs[:, :HD] + pltpu.roll(x, HD // 2, 1) * cs[:, HD:]
+
+    def first_row(g, part, e):
+        m, f = member(g, part, chips)
+        half = (mirror(chip, m, chips) * 2 + e) * 2 + f
+        return half, pl.multiple_of(half * hrows, hrows)
 
     is_end = (me == 0) | (me == last)
 
@@ -384,32 +457,46 @@
         values[pl.ds(0, WINDOW), :] = zero
 
         @pl.loop(0, chips)
-        def _(m):
-            there = mirror(chip, m, chips)
+        def _(g):
             for e in range(2):
-                h = there * 2 + e
-                at = pl.ds(pl.multiple_of(WINDOW + h * rows, rows), rows)
-                scale = row_scale(h)
-                block = kv_ref.at[m, pl.ds(e * rows, rows)]
+                scale = row_scale(g * 2 + e)
+                block = kv_ref.at[g, pl.ds(e * rows, rows)]
                 plain = (block[:, :HD] * scale).astype(BF16).astype(F32)
-                keys[at, :] = rotated(plain, h).astype(BF16)
-                values[at, :] = (block[:, HD:] * scale).astype(BF16)
+                turned = rotated(plain, cs_ref[g * 2 + e]).astype(BF16)
+                value = (block[:, HD:] * scale).astype(BF16)
+                for part in range(2):
+                    _, row = first_row(g, part, e)
+                    at = pl.ds(pl.multiple_of(WINDOW + row, hrows), hrows)
+                    cut = slice(part * hrows, (part + 1) * hrows)
+                    keys[at, :] = turned[cut]
+                    values[at, :] = value[cut]
 
     def attend(j):
         p, t = lax.div(j, tiles), lax.rem(j, tiles)
-        m = chips - 1 - p
-        h = mirror(chip, m, chips) * 2 + end_row
+        g = chips - 1 - p
 
         @pl.when(t == 0)
         def _():
-            mask[...] = jnp.where(allowed_mask(seg_ref[h], rows), 1.0, 0.0)
-
-        at = pl.ds(pl.multiple_of(h * rows, rows), window)
-        scale = row_scale(h)
-        allowed = mask[...] > 0.5
-        to = pl.ds(pl.multiple_of(end_row * rows, rows), rows)
-        for x in range(TILE // HD):
-            query = rotated(q_ref[m * tiles + t, :, x * HD : (x + 1) * HD] * scale, h).astype(BF16)
+            for part in range(2):
+                half, _ = first_row(g, part, end_row)
+                ones = jnp.where(allowed_mask(seg_ref[half], hrows), 1.0, 0.0)
+                mask[part, pl.ds(0, hrows), :] = ones
+                mask[part, pl.ds(hrows, hrows), :] = ones
+            qscale[...] = jnp.broadcast_to(row_scale(g * 2 + end_row), (rows, HD))
+
+        for part in range(2):
+            _, row = first_row(g, part, end_row)
+            at = pl.ds(row, window)
+            cut = slice(part * hrows, (part + 1) * hrows)
+            cs = cs_ref[g * 2 + end_row, cut, :]
+            query = jnp.concatenate(
+                [
+                    rotated(q_ref[g * tiles + t, cut, x * HD : (x + 1) * HD] * qscale[cut, :], cs)
+                    for x in range(TILE // HD)
+                ],
+                axis=0,
+            ).astype(BF16)
+            allowed = mask[part] > 0.5
             scores = lax.dot_general(
                 query, keys[at, :], (((1,), (1,)), ((), ())), preferred_element_type=F32
             ) * HD ** (-0.5)
@@ -417,8 +504,10 @@
             peak = jnp.max(scores, axis=1, keepdims=True)
             expo = jnp.where(allowed, jnp.exp(scores - peak), 0.0)
             weights = (expo / jnp.sum(expo, axis=1, keepdims=True)).astype(BF16)
-            out = jnp.dot(weights, values[at, :], preferred_element_type=F32)
-            head[p, t, to, x * HD : (x + 1) * HD] = out.astype(BF16)
+            out = jnp.dot(weights, values[at, :], preferred_element_type=F32).astype(BF16)
+            to = pl.ds(pl.multiple_of(end_row * rows + part * hrows, hrows), hrows)
+            for x in range(TILE // HD):
+                head[p, t, to, x * HD : (x + 1) * HD] = out[x * hrows : (x + 1) * hrows]
 
     def spread_copy(j, e, peer, sems):
         ref = head.at[lax.div(j, tiles), lax.rem(j, tiles), pl.ds(e * rows, rows)]
@@ -442,10 +531,12 @@
     def pair_copy(v):
         return send_to(acc.at[lax.rem(v, RING), theirs], got.at[v], psem, (v,), ha=partner)
 
-    def peer_copy(v):
-        m = chips - 1 - lax.div(v, wides)
+    def peer_copy(v, part):
+        m, _ = member(chips - 1 - lax.div(v, wides), part, chips)
+        cut = pl.ds(part * hrows, hrows)
         return send_to(
-            stage.at[v], land.at[v], xsem, (v,), ha=mirror(chip, m, chips) * 2 + core
+            stage.at[v, cut], land.at[v, cut], xsem, (v, part),
+            ha=mirror(chip, m, chips) * 2 + core,
         )
 
     def project(v):
@@ -476,7 +567,8 @@
         @pl.when(p < chips - 1)
         def _():
             stage[v] = both.astype(BF16)
-            peer_copy(v).start()
+            for part in range(2):
+                peer_copy(v, part).start()
 
         @pl.when(p == chips - 1)
         def _():
@@ -505,14 +597,17 @@
 
     @pl.loop(0, wides)
     def _(k):
-        total = own[k]
+        halves = [own[k, pl.ds(f * hrows, hrows), :] for f in range(2)]
         for p in range(chips - 1):
-            peer_copy(p * wides + k).wait_recv()
-            total = total + land[p * wides + k].astype(F32)
+            g, v = chips - 1 - p, p * wides + k
+            for part in range(2):
+                peer_copy(v, part).wait_recv()
+                f = part if g == chips - 1 else (g - 1) % 2
+                halves[f] = halves[f] + land[v, pl.ds(part * hrows, hrows), :].astype(F32)
+        total = jnp.concatenate(halves, axis=0)
         at = pl.ds(pl.multiple_of(k * WIDE, WIDE), WIDE)
-        res = (tok_ref[:, at].astype(F32) + total).astype(BF16)
-        res_ref[:, at] = res
-        wide = res.astype(F32)
+        sum_ref[:, at] = total
+        wide = (tok_ref[:, at].astype(F32) + total).astype(BF16).astype(F32)
         square = fold_lanes(wide * wide)
 
         @pl.when(k == 0)
@@ -542,7 +637,8 @@
 
     @pl.loop(0, n_unit - wides)
     def _(v):
-        peer_copy(v).wait_send()
+        for part in range(2):
+            peer_copy(v, part).wait_send()
 
     for v in range(n_unit - RING, n_unit):
         pair_copy(jnp.int32(v)).wait_send()
@@ -551,33 +647,30 @@
     total = sq2[...]
     for d in range(n - 1):
         total = total + lsq2[d]
-    scale_two = column(lax.rsqrt(total[:1] / all_width + EPS))
-
-    @pl.loop(0, wides)
-    def _(k):
-        at = pl.ds(pl.multiple_of(k * WIDE, WIDE), WIDE)
-        wide = res_ref[:, at].astype(F32)
-        ffn_ref[:, at] = (wide * scale_two * gain_ref[:, at].astype(F32)).astype(BF16)
-
-
-def back(q_sum, kv_sum, sq_sum, cs, seg_rows, tokens, gain, w_out, n, n_ha):
+    sqo_ref[...] = total
+
+
+def back(q_sum, kv_sum, sq_sum, cs, seg_rows, tokens, w_out, n, n_ha):
     rows, width = tokens.shape
     cols = w_out.shape[0]
     chips, tiles, wides = n_ha // 2, cols // TILE, width // WIDE
     n_chunk, n_unit = chips * tiles, chips * wides
     vmem, any_ = pl.BlockSpec(memory_space=pltpu.VMEM), pl.BlockSpec(memory_space=pl.ANY)
     dma = pltpu.SemaphoreType.DMA
-    out = jax.ShapeDtypeStruct((rows, width), BF16)
     return pl.pallas_call(
         functools.partial(back_kernel, n, chips, rows, tiles, wides, width * n),
-        out_shape=(out, out),
-        in_specs=[vmem] * 7 + [any_],
+        out_shape=(
+            jax.ShapeDtypeStruct((rows, width), F32),
+            jax.ShapeDtypeStruct((8, rows), F32),
+        ),
+        in_specs=[vmem] * 6 + [any_],
         out_specs=(vmem, vmem),
         scratch_shapes=[
             pltpu.VMEM((wides, cols, WIDE), BF16),
             pltpu.VMEM((WINDOW + n_ha * rows, HD), BF16),
             pltpu.VMEM((WINDOW + n_ha * rows, HD), BF16),
-            pltpu.VMEM((rows, WINDOW + rows), F32),
+            pltpu.VMEM((2, rows, WINDOW + rows // 2), F32),
+            pltpu.VMEM((rows, HD), F32),
             pltpu.VMEM((chips, tiles, 2 * rows, TILE), BF16),
             pltpu.VMEM((RING, 2 * rows, WIDE), F32),
             pltpu.VMEM((n_unit, rows, WIDE), F32),
@@ -591,13 +684,13 @@
             dma((2, n_chunk)),
             dma((2, n_chunk)),
             dma((2, n_unit)),
-            dma((2, n_unit - wides)),
+            dma((2, n_unit - wides, 2)),
             dma((2, n - 1)),
         ],
         compiler_params=pltpu.CompilerParams(
             collective_id=1, has_side_effects=True, vmem_limit_bytes=60 << 20
         ),
-    )(q_sum, kv_sum, sq_sum, cs, seg_rows, tokens, gain, w_out)
+    )(q_sum, kv_sum, sq_sum, cs, seg_rows, tokens, w_out)
 
 
 def on_device(tokens, gain_attn, w_query, w_key, w_value, w_out, gain_ffn, segment_ids):
@@ -605,15 +698,23 @@
     n_wa = lax.axis_size("wa")
     n_ha = lax.axis_size("ha")
     padded = jnp.pad(segment_ids, (WINDOW, 0), constant_values=-1).astype(F32)
-    seg_rows = jnp.stack([padded[None, h * rows : (h + 1) * rows + WINDOW] for h in range(n_ha)])
+    half = rows // 2
+    seg_rows = jnp.stack(
+        [padded[None, k * half : (k + 1) * half + WINDOW] for k in range(2 * n_ha)]
+    )
     q_sum, kv_sum, sq_sum, cs = front(
         tokens, gain_attn.reshape(1, width), w_query, w_key, w_value, seg_rows, rope_rows(),
         n_wa, n_ha,
     )
-    return back(
-        q_sum, kv_sum, sq_sum, cs, seg_rows, tokens, gain_ffn.reshape(1, width), w_out,
-        n_wa, n_ha,
+    attended, square_two = back(
+        q_sum, kv_sum, sq_sum, cs, seg_rows, tokens, w_out, n_wa, n_ha
     )
+    residual_out = (tokens.astype(F32) + attended).astype(BF16)
+    scale_two = lax.rsqrt(square_two[0] / (width * n_wa) + EPS)
+    ffn_input = (
+        residual_out.astype(F32) * scale_two[:, None] * gain_ffn.astype(F32)
+    ).astype(BF16)
+    return (residual_out, ffn_input)
 
 
 def solution(mesh):

time: 259 us -> 192 us (0.74)
  Pallas kernels: 249 us -> 183 us
  local copies, waits for them, and re-layouts: 7.27 us -> 1.54 us
  other arithmetic: 2.09 us -> 6.13 us
    pallas_call x1, Pallas kernels: 153 us -> 94.4 us  [front(): pl.pallas_call(functools.partial(front_kernel, n, chips, rows, tiles, n_h...]
    pallas_call x1, Pallas kernels: 95.5 us -> 88.8 us  [back(): pl.pallas_call(functools.partial(back_kernel, n, chips, rows, tiles, wide...]
    unnamed x11 -> x21, local copies, waits for them, and re-layouts: 4.64 us -> 0.15 us
    convert_element_type x0 -> x2, other arithmetic: none -> 3.37 us  [the longest x1 3.36 us: on_device(): ffn_input = (residual_out.astype(F32) * scale_two[:, None] * gain_ffn.ast...]
where the time goes in v2:
time: 192 us
  Pallas kernels  183 us (95%)
  other arithmetic  6.13 us (3%)
    pallas_call x1, Pallas kernels, front(): pl.pallas_call(functools.partial(front_kernel, n, chips, rows, tiles, n_h...  94.4 us
    pallas_call x1, Pallas kernels, back(): pl.pallas_call(functools.partial(back_kernel, n, chips, rows, tiles, wide...  88.8 us

profile of v2, /device:TPU:0, one launch (start us, length us, event | category | flops | bytes accessed | tf_op | source)
XLA Modules:
  0.0 191.6 jit_solution(4955402901233147087)
XLA Ops:
  0.6 0.7 pad_convert_fusion
  1.3 0.1 fusion.3
  1.6 0.0 copy-start.1
  1.6 0.5 fusion.1
  2.1 0.9 pad_maximum_fusion.rope_ref
  3.0 1.3 reshape.26.gain_ref
  4.3 0.0 copy-done.1
  4.3 94.4 %shard_map.95 = (f32[32,128,256]{2,1,0:T(8,128)}, f32[4,256,256]{2,1,0:T(8,128)}, f32[8,128]{1,0:T(8,128)}, f32[8,128,256]{2,1,0:T(8,128)}) custom-call(bf16[128,4096]{1,0:T(8,128)(2,1)} %tok_ref.1, bf16[1,4096]{1,0:T(2,128)(2,1)} %reshape.26.gain_ref, bf16[4096,2048]{1,0:T(8,128)(2,1)} %wq_hbm.1, bf16[4096,1024]{1,0:T(8,128)(2,1)} %wk_hbm.1, ...), custom_call_target="tpu_custom_call" | custom-call | tf_op jit(solution)/shard_map/pallas_call | solution.py:374
  98.8 0.0 copy-start.2
  98.8 0.0 copy-start
  98.8 88.8 %shard_map.96 = (f32[128,4096]{1,0:T(8,128)}, f32[8,128]{1,0:T(8,128)}) custom-call(f32[32,128,256]{2,1,0:T(8,128)} %get-tuple-element.8.q_ref, f32[4,256,256]{2,1,0:T(8,128)} %get-tuple-element.9.kv_ref, f32[8,128]{1,0:T(8,128)} %get-tuple-element.10.sq_ref, f32[8,128,256]{2,1,0:T(8,128)} %get-tuple-element.11.cs_ref, f32[16,1,320]{2,1,0:T(1,128)} %copy-done.1, ...), custom_call_target="tpu_custom_call" | custom-call | tf_op jit(solution)/shard_map/pallas_call | solution.py:660
  187.6 0.7 rsqrt_bitcast_fusion
  188.3 0.0 copy-done.2
  188.3 0.0 copy-done
  188.3 3.4 %multiply_convert_fusion = (bf16[128,4096]{1,0:T(8,128)(2,1)}, bf16[128,4096]{1,0:T(8,128)(2,1)}) fusion(f32[4096]{0:T(1024)S(1)} %convert_element_type.22, f32[128]{0:T(128)S(1)} %rsqrt_bitcast_fusion, f32[128,4096]{1,0:T(8,128)} %get-tuple-element.12, bf16[128,4096]{1,0:T(8,128)(2,1)S(1)} %copy-done), kind=kLoop, calls=%fused_computation | loop fusion | flops 3670016 | bytes 5259776 | tf_op jit(solution)/shard_map/convert_element_type | solution.py:716
  (18 shorter events, 0.2 us)
Async XLA Ops:
  1.6 2.7 %copy-start.1 = (f32[16,1,320]{2,1,0:T(1,128)}, f32[16,1,320]{2,1,0:T(1,128)S(1)}, u32[]{:S(2)}) copy-start(f32[16,1,320]{2,1,0:T(1,128)S(1)} %constant_dynamic-update-slice_fusion.seg_ref) | copy-start | bytes 61444
  98.8 89.5 %copy-start.2 = (bf16[4096]{0:T(1024)(128)(2,1)S(1)}, bf16[4096]{0:T(1024)(128)(2,1)}, u32[]{:S(2)}) copy-start(bf16[4096]{0:T(1024)(128)(2,1)} %param.14) | copy-start | bytes 24580
  98.8 89.5 %copy-start = (bf16[128,4096]{1,0:T(8,128)(2,1)S(1)}, bf16[128,4096]{1,0:T(8,128)(2,1)}, u32[]{:S(2)}) copy-start(bf16[128,4096]{1,0:T(8,128)(2,1)} %tok_ref.1) | copy-start | bytes 3145732

commit v3 on v2

v3 whole, which is shorter than its diff:
```python
import functools

import jax
import jax.numpy as jnp
from jax import lax
from jax.experimental import pallas as pl
from jax.experimental.pallas import tpu as pltpu
from jax.sharding import PartitionSpec as P

KVH = 8
HD = 128
WINDOW = 256
EPS = 1e-05
TILE = 256
WIDE = 512
SKEW = 3
SPREAD_SKEW = 3
LEVELS = 32766.0
FORWARD = 2
RING = 4
DEEP = 8
F32 = jnp.float32
BF16 = jnp.bfloat16


def rope_rows():
    half = HD // 2
    inverse = 500000.0 ** (-(jnp.arange(half, dtype=F32) * 2.0 / HD))
    angle = jnp.arange(WINDOW, dtype=F32)[:, None] * inverse[None, :]
    cosine, sine = jnp.cos(angle), jnp.sin(angle)
    return jnp.concatenate([cosine, cosine, -sine, sine], axis=1)


def mirror(a, m, size):
    total, bit = 0, 1
    while bit < size:
        total = total + lax.rem(lax.div(a, bit) + lax.div(m, bit), 2) * bit
        bit *= 2
    return total


def member(g, sub, chips):
    edge = (g == 0) | (g == chips - 1)
    low = lax.div(g - 1, 2) * 2 + 1
    return jnp.where(edge, g, low + sub), jnp.where(edge, sub, lax.rem(g - 1, 2))


def place(m, f, chips):
    edge = (m == 0) | (m == chips - 1)
    low = lax.div(m - 1, 2) * 2 + 1
    return jnp.where(edge, m, low + f), jnp.where(edge, f, lax.rem(m - 1, 2))


def send_to(src, dst, sems, at, **peer):
    return pltpu.make_async_remote_copy(
        src_ref=src,
        dst_ref=dst,
        send_sem=sems.at[(0,) + at],
        recv_sem=sems.at[(1,) + at],
        device_id=peer,
        device_id_type=pl.DeviceIdType.MESH,
    )


def greet(n, chips, me, chip, core):
    barrier = pltpu.get_barrier_semaphore()

    def signal(**peer):
        pl.semaphore_signal(
            barrier, inc=1, device_id=peer, device_id_type=pl.DeviceIdType.MESH
        )

    for d in range(1, n):
        signal(wa=lax.rem(me + d, n))
    for m in range(1, chips):
        signal(ha=mirror(chip, jnp.int32(m), chips) * 2 + core)
    signal(ha=chip * 2 + 1 - core)
    pl.semaphore_wait(barrier, n + chips - 1)


def column(row):
    r = row.shape[1]
    a = lax.broadcasted_iota(jnp.int32, (r, r), 0)
    b = lax.broadcasted_iota(jnp.int32, (r, r), 1)
    return jnp.sum(jnp.where(a == b, jnp.broadcast_to(row, (r, r)), 0.0), axis=1, keepdims=True)


def as_row(col):
    r = col.shape[0]
    a = lax.broadcasted_iota(jnp.int32, (r, r), 0)
    b = lax.broadcasted_iota(jnp.int32, (r, r), 1)
    return jnp.sum(jnp.where(a == b, jnp.broadcast_to(col, (r, r)), 0.0), axis=0, keepdims=True)


def encode(x, code, steps, rows):
    for i in range(x.shape[0] // rows):
        for y in range(TILE // HD):
            part = x[i * rows : (i + 1) * rows, y * HD : (y + 1) * HD]
            top = jnp.maximum(jnp.max(jnp.abs(part), axis=1, keepdims=True), 1e-30)
            whole = jnp.round(part * (LEVELS / top)).astype(jnp.int32)
            code[i * rows : (i + 1) * rows, y * HD : (y + 1) * HD] = whole.astype(jnp.int16)
            k = i * 2 + y
            steps[k : k + 1, :] = as_row(top * (1.0 / LEVELS))


def decode(code, steps, rows):
    blocks = []
    for i in range(code.shape[0] // rows):
        line = []
        for y in range(TILE // HD):
            part = code[i * rows : (i + 1) * rows, y * HD : (y + 1) * HD]
            k = i * 2 + y
            line.append(part.astype(jnp.int32).astype(F32) * column(steps[k : k + 1, :]))
        blocks.append(jnp.concatenate(line, axis=1))
    return jnp.concatenate(blocks, axis=0)


def lane_sums(block):
    ones = jnp.ones((8, block.shape[1]), F32)
    return lax.dot_general(
        ones, block, (((1,), (1,)), ((), ())), precision=lax.Precision.HIGHEST,
        preferred_element_type=F32,
    )


def fold_lanes(x):
    total = x[:, :128]
    for g in range(1, x.shape[1] // 128):
        total = total + x[:, g * 128 : (g + 1) * 128]
    return total


def allowed_mask(seg_row, rows):
    keys = seg_row.shape[1]
    q_seg = column(seg_row[:, keys - rows :])
    q_at = lax.broadcasted_iota(jnp.int32, (rows, keys), 0) + (keys - rows)
    k_at = lax.broadcasted_iota(jnp.int32, (rows, keys), 1)
    return (q_seg == seg_row) & (k_at <= q_at)


def plan(n, chips, tiles, wides):
    units = tiles + 1
    start = 0
    for p in range(chips):
        g = (p + 1) % chips
        start = max(start, (g + 1) * units + SKEW * (n - 1) - p * tiles)
    start = max(start, (chips - 1) * units + SKEW * (n - 1) + 1)
    lag = max(0, tiles - wides) * chips + tiles + SPREAD_SKEW * (n - 1)
    return start, lag


def layer_kernel(
    n, chips, rows, tiles, wides, per_head, all_width,
    tok_hbm, gain_ref, wq_hbm, wk_hbm, wv_hbm, seg_ref, rope_ref, tok_ref, wo_hbm,
    sum_ref, scale_ref,
    tok, scaled, w, parts, qr, ql, kr, kl, er, el, cs, sqp, sqs, lsq,
    keys, values, mask, qscale, head, acc, got, own, sq2, lsq2,
    wsem, tsem, same_sem, pair_sem, rsem, lsem, resem, lesem, ssem,
    osem, srsem, slsem, psem, xsem, s2sem, free_sem, credit_sem,
):
    me, ha = lax.axis_index("wa"), lax.axis_index("ha")
    core, chip = lax.rem(ha, 2), lax.div(ha, 2)
    last = n - 1
    units = tiles + 1
    count = chips * units
    n_chunk, n_unit = chips * tiles, chips * wides
    start, lag = plan(n, chips, tiles, wides)
    hrows = rows // 2
    window = WINDOW + hrows
    cols = tiles * TILE
    fold = w.shape[1] // cols
    own_at = pl.multiple_of(core * rows, rows)
    kv_at = pl.multiple_of(lax.div(ha, per_head) * HD, HD)
    partner = chip * 2 + 1 - core
    mine = pl.ds(own_at, rows)
    theirs = pl.ds(pl.multiple_of((1 - core) * rows, rows), rows)
    right, left = jnp.minimum(me + 1, last), jnp.maximum(me - 1, 0)
    end_row = jnp.where(me == last, 1, 0)
    is_end = (me == 0) | (me == last)

    def w_copies(u):
        if u == 0:
            return [
                pltpu.make_async_copy(
                    wk_hbm.at[:, pl.ds(kv_at, HD)], w.at[0, :, pl.ds(0, HD)], wsem.at[0]
                ),
                pltpu.make_async_copy(
                    wv_hbm.at[:, pl.ds(kv_at, HD)], w.at[0, :, pl.ds(HD, HD)], wsem.at[1]
                ),
            ]
        return [
            pltpu.make_async_copy(
                wq_hbm.at[:, pl.ds((u - 1) * TILE, TILE)], w.at[u], wsem.at[u + 1]
            )
        ]

    def wo_copy(c):
        return pltpu.make_async_copy(
            wo_hbm.at[:, pl.ds(c * TILE, TILE)],
            w.at[c // fold, pl.ds((c % fold) * cols, cols)],
            osem.at[c],
        )

    n_wo = wides * (WIDE // TILE)

    own_copy = pltpu.make_async_copy(tok_hbm, tok.at[0, mine], tsem)
    own_copy.start()
    for u in range(units):
        for copy in w_copies(u):
            copy.start()
    greet(n, chips, me, chip, core)

    def half_rows(f):
        return pl.ds(pl.multiple_of(f * hrows, hrows), hrows)

    def spot(m, f):
        g, part = place(m, f, chips)
        return tok.at[g, pl.ds(pl.multiple_of(own_at + part * hrows, hrows), hrows)]

    def same_copy(m, f):
        return send_to(
            tok_hbm.at[half_rows(f)], spot(m, f), same_sem, (m, f),
            ha=mirror(chip, m, chips) * 2 + core,
        )

    def pair_copy(m, f, first):
        src = tok_hbm.at[half_rows(f)] if first else spot(m, f)
        return send_to(src, spot(m, f), pair_sem, (m, f), ha=partner)

    for f in range(2):
        pair_copy(jnp.int32(0), f, True).start()
    for f in range(2):
        for m in range(1, min(3, chips)):
            same_copy(jnp.int32(m), f).start()

    def peers(src, dst, sems):
        return [
            send_to(src, dst.at[d - 1], sems, (d - 1,), wa=lax.rem(me + d, n))
            for d in range(1, n)
        ]

    small, small_two = peers(sqs, lsq, ssem), peers(sq2, lsq2, s2sem)

    def prepare(g):
        @pl.loop(0, 2 * rows // 16)
        def _(i):
            at = pl.ds(pl.multiple_of(i * 16, 16), 16)
            x = tok[g, at, :].astype(F32)
            scaled[at, :] = (x * gain_ref[...].astype(F32)).astype(BF16)
            sqp[at, :] = fold_lanes(x * x)

        for e in range(2):
            sqs[pl.ds(g * 2 + e, 1), :] = lane_sums(sqp[pl.ds(e * rows, rows), :])[:1]

    def tables(g):
        for e in range(2):
            for part in range(2):
                m, f = member(g, part, chips)
                allowed = allowed_mask(seg_ref[(mirror(chip, m, chips) * 2 + e) * 2 + f], hrows)
                at = jnp.sum(jnp.where(allowed, 1.0, 0.0), axis=1, keepdims=True) - 1.0
                lanes = lax.broadcasted_iota(jnp.int32, (hrows, WINDOW), 1)
                pick = jnp.where(lanes == at.astype(jnp.int32), 1.0, 0.0)
                cs[g * 2 + e, part * hrows : (part + 1) * hrows, :] = jnp.dot(
                    pick, rope_ref[...], precision=lax.Precision.HIGHEST,
                    preferred_element_type=F32,
                )

    def code_copies(land, steps, sems, step_sems, j, peer):
        return (
            send_to(land, land, sems, (j,), wa=peer),
            send_to(steps, steps, step_sems, (j,), wa=peer),
        )

    def handle(pos, peer, part, land, steps, sems, step_sems, j):
        copies = code_copies(land, steps, sems, step_sems, j, peer)

        @pl.when(pos == 0)
        def _():
            encode(part[...], land, steps, rows)

        @pl.when(pos > 0)
        def _():
            for copy in copies:
                copy.wait_recv()

        @pl.when((pos > 0) & (pos < last))
        def _():
            encode(decode(land, steps, rows) + part[...], land, steps, rows)

        @pl.when(pos < last)
        def _():
            for copy in copies:
                copy.start()

        @pl.when(pos == last)
        def _():
            part[...] = decode(land, steps, rows) + part[...]

    def reduce_step(s, pos, peer, e, q_land, k_land, steps, sems, step_sems):
        j = s - SKEW * pos

        @pl.when((j >= 0) & (j < count))
        def _():
            g, u = lax.div(j, units), lax.rem(j, units)

            @pl.when(u == 0)
            def _():
                handle(
                    pos, peer, parts.at[j], k_land.at[g], steps.at[j], sems, step_sems, j
                )

            @pl.when(u > 0)
            def _():
                jq = g * tiles + u - 1
                part = parts.at[j, pl.ds(e * rows, rows)]
                handle(pos, peer, part, q_land.at[jq], steps.at[j], sems, step_sems, j)

    def front_step(s):
        g, u = lax.div(s, units), lax.rem(s, units)

        @pl.when(s < count)
        def _():
            @pl.when(u == 0)
            def _():
                @pl.when(g == 0)
                def _():
                    own_copy.wait()

                for part in range(2):
                    pair_copy(*member(g, part, chips), False).wait_recv()
                prepare(g)

                @pl.when(g == chips - 1)
                def _():
                    for copy in small:
                        copy.start()

            for v in range(units):

                @pl.when(s == v)
                def _():
                    for copy in w_copies(v):
                        copy.wait()

            parts[s] = jnp.dot(scaled[...], w[u], preferred_element_type=F32)

        @pl.when(s == count)
        def _():
            for c in range(n_wo):
                wo_copy(c).start()

        reduce_step(s, me, right, 1, qr, kr, er, rsem, resem)
        reduce_step(s, last - me, left, 0, ql, kl, el, lsem, lesem)

        @pl.when((s < count) & (u == 1))
        def _():
            tables(g)

        @pl.when((u == max(0, units - FORWARD)) & (g + 1 < chips))
        def _():
            @pl.when(g + 3 < chips)
            def _():
                for f in range(2):
                    same_copy(g + 3, f).start()

            for part in range(2):
                m, f = member(g + 1, part, chips)
                same_copy(m, f).wait_recv()
                pair_copy(m, f, False).start()

    def drain(j, pos, peer, q_land, k_land, steps, sems, step_sems):
        g, u = lax.div(j, units), lax.rem(j, units)

        @pl.when((pos < last) & (u == 0))
        def _():
            for copy in code_copies(k_land.at[g], steps.at[j], sems, step_sems, j, peer):
                copy.wait_send()

        @pl.when((pos < last) & (u > 0))
        def _():
            jq = g * tiles + u - 1
            for copy in code_copies(q_land.at[jq], steps.at[j], sems, step_sems, j, peer):
                copy.wait_send()

    def group(p):
        return lax.rem(p + 1, chips)

    def row_scale(k):
        return column(lax.rsqrt(sqs[pl.ds(k, 1), :] / all_width + EPS))

    def rotated(x, turn):
        return x * turn[:, :HD] + pltpu.roll(x, HD // 2, 1) * turn[:, HD:]

    def first_row(g, part, e):
        m, f = member(g, part, chips)
        half = (mirror(chip, m, chips) * 2 + e) * 2 + f
        return half, pl.multiple_of(half * hrows, hrows)

    def settle():
        for m in range(chips):
            for f in range(2):
                pair_copy(jnp.int32(m), f, False).wait_send()
                if m:
                    same_copy(jnp.int32(m), f).wait_send()
        for m in range(1, chips):
            pl.semaphore_signal(
                free_sem, inc=1,
                device_id={"ha": mirror(chip, jnp.int32(m), chips) * 2 + core},
                device_id_type=pl.DeviceIdType.MESH,
            )
        for copy in small:
            copy.wait()
        total = sqs[...]
        for d in range(n - 1):
            total = total + lsq[d]
        sqs[...] = total

        @pl.when(is_end)
        def _():
            zero = jnp.zeros((WINDOW, HD), BF16)
            keys[pl.ds(0, WINDOW), :] = zero
            values[pl.ds(0, WINDOW), :] = zero

            @pl.loop(0, chips)
            def _(g):
                for e in range(2):
                    scale = row_scale(g * 2 + e)
                    block = parts.at[g * units, pl.ds(e * rows, rows)]
                    plain = (block[:, :HD] * scale).astype(BF16).astype(F32)
                    turned = rotated(plain, cs[g * 2 + e]).astype(BF16)
                    value = (block[:, HD:] * scale).astype(BF16)
                    for part in range(2):
                        _, row = first_row(g, part, e)
                        at = pl.ds(pl.multiple_of(WINDOW + row, hrows), hrows)
                        cut = slice(part * hrows, (part + 1) * hrows)
                        keys[at, :] = turned[cut]
                        values[at, :] = value[cut]

    def attend(j):
        p, t = lax.div(j, tiles), lax.rem(j, tiles)
        g = group(p)

        @pl.when(t == 0)
        def _():
            for part in range(2):
                half, _ = first_row(g, part, end_row)
                ones = jnp.where(allowed_mask(seg_ref[half], hrows), 1.0, 0.0)
                mask[part, pl.ds(0, hrows), :] = ones
                mask[part, pl.ds(hrows, hrows), :] = ones
            qscale[...] = jnp.broadcast_to(row_scale(g * 2 + end_row), (rows, HD))

        for part in range(2):
            _, row = first_row(g, part, end_row)
            at = pl.ds(row, window)
            cut = slice(part * hrows, (part + 1) * hrows)
            to = pl.ds(pl.multiple_of(end_row * rows + part * hrows, hrows), hrows)
            turn = cs[g * 2 + end_row, cut, :]
            query = jnp.concatenate(
                [
                    rotated(
                        parts[g * units + 1 + t, to, x * HD : (x + 1) * HD] * qscale[cut, :], turn
                    )
                    for x in range(TILE // HD)
                ],
                axis=0,
            ).astype(BF16)
            allowed = mask[part] > 0.5
            scores = lax.dot_general(
                query, keys[at, :], (((1,), (1,)), ((), ())), preferred_element_type=F32
            ) * HD ** (-0.5)
            scores = jnp.where(allowed, scores, -1e30)
            peak = jnp.max(scores, axis=1, keepdims=True)
            expo = jnp.where(allowed, jnp.exp(scores - peak), 0.0)
            weights = (expo / jnp.sum(expo, axis=1, keepdims=True)).astype(BF16)
            out = jnp.dot(weights, values[at, :], preferred_element_type=F32).astype(BF16)
            for x in range(TILE // HD):
                head[p, t, to, x * HD : (x + 1) * HD] = out[x * hrows : (x + 1) * hrows]

    def spread_copy(j, e, peer, sems):
        ref = head.at[lax.div(j, tiles), lax.rem(j, tiles), pl.ds(e * rows, rows)]
        return send_to(ref, ref, sems, (j,), wa=peer)

    def spread_step(s, pos, peer, e, sems):
        j = s - SPREAD_SKEW * pos

        @pl.when((j >= 0) & (j < n_chunk))
        def _():
            copy = spread_copy(j, e, peer, sems)

            @pl.when(pos > 0)
            def _():
                copy.wait_recv()

            @pl.when(pos < last)
            def _():
                copy.start()

    def swap_copy(v):
        return send_to(
            acc.at[lax.rem(v, RING), theirs], got.at[lax.rem(v, DEEP)], psem, (v,), ha=partner
        )

    def stage(v, part):
        p, k = lax.div(v, wides), lax.rem(v, wides)
        at = pl.ds(pl.multiple_of(k * WIDE, WIDE), WIDE)
        return tok.at[p, pl.ds(rows + part * hrows, hrows), at]

    def land(v, part):
        p, k = lax.div(v, wides), lax.rem(v, wides)
        at = pl.ds(pl.multiple_of(k * WIDE, WIDE), WIDE)
        return tok.at[p, pl.ds(part * hrows, hrows), at]

    def peer_copy(v, part):
        m, _ = member(group(lax.div(v, wides)), part, chips)
        return send_to(
            stage(v, part), land(v, part), xsem, (v, part), ha=mirror(chip, m, chips) * 2 + core
        )

    def project(v):
        p, k = lax.div(v, wides), lax.rem(v, wides)

        @pl.when(v == 0)
        def _():
            for c in range(n_wo):
                wo_copy(c).wait()

        @pl.when(v >= RING)
        def _():
            swap_copy(v - RING).wait_send()

        block = jnp.concatenate([head[p, t] for t in range(tiles)], axis=1)
        for y in range(WIDE // TILE):
            c = k * (WIDE // TILE) + y
            deep = pl.ds(pl.multiple_of(lax.rem(c, fold) * cols, cols), cols)
            acc[lax.rem(v, RING), :, y * TILE : (y + 1) * TILE] = jnp.dot(
                block, w[lax.div(c, fold), deep, :], preferred_element_type=F32
            )

        @pl.when(v >= DEEP)
        def _():
            pl.semaphore_wait(credit_sem, 1)

        swap_copy(v).start()

    def combine(v):
        p, k = lax.div(v, wides), lax.rem(v, wides)
        swap_copy(v).wait_recv()
        both = acc[lax.rem(v, RING), mine, :] + got[lax.rem(v, DEEP)]

        @pl.when(v + DEEP < n_unit)
        def _():
            pl.semaphore_signal(
                credit_sem, inc=1, device_id={"ha": partner},
                device_id_type=pl.DeviceIdType.MESH,
            )

        @pl.when(v == 0)
        def _():
            pl.semaphore_wait(free_sem, chips - 1)

        @pl.when(p < chips - 1)
        def _():
            for part in range(2):
                stage(v, part)[...] = both[part * hrows : (part + 1) * hrows].astype(BF16)
                peer_copy(v, part).start()

        @pl.when(p == chips - 1)
        def _():
            own[k] = both

    @pl.loop(0, start + lag + n_unit + 1)
    def _(s):
        @pl.when(s < count + SKEW * last)
        def _():
            front_step(s)

        @pl.when(s == start)
        def _():
            settle()

        r = s - start

        @pl.when(r >= 0)
        def _():
            @pl.when(is_end & (r < n_chunk))
            def _():
                attend(r)

            spread_step(r, me, right, 0, srsem)
            spread_step(r, last - me, left, 1, slsem)

        v = r - lag

        @pl.when((v >= 0) & (v < n_unit))
        def _():
            project(v)

        @pl.when(v >= 1)
        def _():
            combine(v - 1)

    @pl.loop(0, wides)
    def _(k):
        halves = [own[k, pl.ds(f * hrows, hrows), :] for f in range(2)]
        for p in range(chips - 1):
            g, v = p + 1, p * wides + k
            for part in range(2):
                peer_copy(v, part).wait_recv()
                f = part if g == chips - 1 else (g - 1) % 2
                halves[f] = halves[f] + land(v, part)[...].astype(F32)
        total = jnp.concatenate(halves, axis=0)
        at = pl.ds(pl.multiple_of(k * WIDE, WIDE), WIDE)
        sum_ref[:, at] = total
        wide = (tok_ref[:, at].astype(F32) + total).astype(BF16).astype(F32)
        square = fold_lanes(wide * wide)

        @pl.when(k == 0)
        def _():
            sqp[pl.ds(0, rows), :] = square

        @pl.when(k > 0)
        def _():
            sqp[pl.ds(0, rows), :] = sqp[pl.ds(0, rows), :] + square

    sq2[...] = lane_sums(sqp[pl.ds(0, rows), :])
    for copy in small_two:
        copy.start()

    @pl.loop(0, count)
    def _(j):
        drain(j, me, right, qr, kr, er, rsem, resem)
        drain(j, last - me, left, ql, kl, el, lsem, lesem)

    @pl.loop(0, n_chunk)
    def _(j):
        @pl.when(me < last)
        def _():
            spread_copy(j, 0, right, srsem).wait_send()

        @pl.when(me > 0)
        def _():
            spread_copy(j, 1, left, slsem).wait_send()

    @pl.loop(0, n_unit - wides)
    def _(v):
        for part in range(2):
            peer_copy(v, part).wait_send()

    for v in range(n_unit - RING, n_unit):
        swap_copy(jnp.int32(v)).wait_send()
    for copy in small_two:
        copy.wait()
    total = sq2[...]
    for d in range(n - 1):
        total = total + lsq2[d]
    scale_ref[...] = jnp.broadcast_to(
        column(lax.rsqrt(total[:1] / all_width + EPS)), scale_ref.shape
    )


def layer(tokens, gain, w_query, w_key, w_value, seg_rows, rope, w_out, n, n_ha):
    rows, width = tokens.shape
    cols = w_query.shape[1]
    chips, tiles, wides = n_ha // 2, cols // TILE, width // WIDE
    units = tiles + 1
    count = chips * units
    n_chunk, n_unit = chips * tiles, chips * wides
    vmem, any_ = pl.BlockSpec(memory_space=pltpu.VMEM), pl.BlockSpec(memory_space=pl.ANY)
    dma, reg = pltpu.SemaphoreType.DMA, pltpu.SemaphoreType.REGULAR
    i16 = jnp.int16
    return pl.pallas_call(
        functools.partial(
            layer_kernel, n, chips, rows, tiles, wides, n_ha // KVH, width * n
        ),
        out_shape=(
            jax.ShapeDtypeStruct((rows, width), F32),
            jax.ShapeDtypeStruct((rows, 128), F32),
        ),
        in_specs=[any_, vmem, any_, any_, any_, vmem, vmem, vmem, any_],
        out_specs=(vmem, vmem),
        scratch_shapes=[
            pltpu.VMEM((chips, 2 * rows, width), BF16),
            pltpu.VMEM((2 * rows, width), BF16),
            pltpu.VMEM((units, width, TILE), BF16),
            pltpu.VMEM((count, 2 * rows, TILE), F32),
            pltpu.VMEM((chips * tiles, rows, TILE), i16),
            pltpu.VMEM((chips * tiles, rows, TILE), i16),
            pltpu.VMEM((chips, 2 * rows, TILE), i16),
            pltpu.VMEM((chips, 2 * rows, TILE), i16),
            pltpu.VMEM((count, 4, rows), F32),
            pltpu.VMEM((count, 4, rows), F32),
            pltpu.VMEM((n_ha, rows, 2 * HD), F32),
            pltpu.VMEM((2 * rows, 128), F32),
            pltpu.VMEM((n_ha, rows), F32),
            pltpu.VMEM((n - 1, n_ha, rows), F32),
            pltpu.VMEM((WINDOW + n_ha * rows, HD), BF16),
            pltpu.VMEM((WINDOW + n_ha * rows, HD), BF16),
            pltpu.VMEM((2, rows, WINDOW + rows // 2), F32),
            pltpu.VMEM((rows, HD), F32),
            pltpu.VMEM((chips, tiles, 2 * rows, TILE), BF16),
            pltpu.VMEM((RING, 2 * rows, WIDE), F32),
            pltpu.VMEM((DEEP, rows, WIDE), F32),
            pltpu.VMEM((wides, rows, WIDE), F32),
            pltpu.VMEM((8, rows), F32),
            pltpu.VMEM((n - 1, 8, rows), F32),
            dma((units + 1,)),
            dma,
            dma((2, chips, 2)),
            dma((2, chips, 2)),
            dma((2, count)),
            dma((2, count)),
            dma((2, count)),
            dma((2, count)),
            dma((2, n - 1)),
            dma((wides * (WIDE // TILE),)),
            dma((2, n_chunk)),
            dma((2, n_chunk)),
            dma((2, n_unit)),
            dma((2, n_unit - wides, 2)),
            dma((2, n - 1)),
            reg,
            reg,
        ],
        compiler_params=pltpu.CompilerParams(
            collective_id=0, has_side_effects=True, vmem_limit_bytes=63 << 20
        ),
    )(tokens, gain, w_query, w_key, w_value, seg_rows, rope, tokens, w_out)


def on_device(tokens, gain_attn, w_query, w_key, w_value, w_out, gain_ffn, segment_ids):
    rows, width = tokens.shape
    n_wa = lax.axis_size("wa")
    n_ha = lax.axis_size("ha")
    padded = jnp.pad(segment_ids, (WINDOW, 0), constant_values=-1).astype(F32)
    half = rows // 2
    seg_rows = jnp.stack(
        [padded[None, k * half : (k + 1) * half + WINDOW] for k in range(2 * n_ha)]
    )
    attended, scale_two = layer(
        tokens, gain_attn.reshape(1, width), w_query, w_key, w_value, seg_rows, rope_rows(),
        w_out, n_wa, n_ha,
    )
    residual_out = (tokens.astype(F32) + attended).astype(BF16)
    ffn_input = (
        residual_out.astype(F32) * scale_two[:, :1] * gain_ffn.astype(F32)
    ).astype(BF16)
    return (residual_out, ffn_input)


def solution(mesh):
    in_specs = (
        P("ha", "wa"),
        P("wa"),
        P("wa", "ha"),
        P("wa", None),
        P("wa", None),
        P("ha", "wa"),
        P("wa"),
        P(),
    )
    out_specs = (P("ha", "wa"), P("ha", "wa"))
    return jax.shard_map(
        on_device, mesh=mesh, in_specs=in_specs, out_specs=out_specs, check_vma=False
    )
```

time: 192 us -> 180 us (0.938)
  Pallas kernels: 183 us -> 170 us
    pallas_call x2 -> x1, Pallas kernels: 183 us -> 170 us  [layer(): pl.pallas_call(functools.partial(layer_kernel, n, chips, rows, tiles, wid...]
where the time goes in v3:
time: 180 us
  Pallas kernels  170 us (94%)
  other arithmetic  6.42 us (4%)
  local copies, waits for them, and re-layouts  2.47 us (1%)
    pallas_call x1, Pallas kernels, layer(): pl.pallas_call(functools.partial(layer_kernel, n, chips, rows, tiles, wid...  170 us
    convert_element_type x1, other arithmetic, on_device(): ffn_input = (residual_out.astype(F32) * scale_two[:, :1] * gain_ffn.astyp...  3.63 us

profile of v3, /device:TPU:0, one launch (start us, length us, event | category | flops | bytes accessed | tf_op | source)
XLA Modules:
  0.0 179.9 jit_solution(270148581623996861)
XLA Ops:
  0.6 0.7 pad_convert_fusion
  1.3 1.3 reshape.14.gain_ref
  2.6 0.7 convert_element_type.22
  3.3 0.1 fusion.3
  3.6 0.0 copy-start
  3.6 0.5 fusion.1
  4.1 0.9 pad_maximum_fusion.rope_ref
  5.0 0.0 copy-done
  5.0 170.3 %shard_map.95 = (f32[128,4096]{1,0:T(8,128)}, f32[128,128]{1,0:T(8,128)}) custom-call(bf16[128,4096]{1,0:T(8,128)(2,1)} %tok_ref.1, bf16[1,4096]{1,0:T(2,128)(2,1)} %reshape.14.gain_ref, bf16[4096,2048]{1,0:T(8,128)(2,1)} %wq_hbm.1, bf16[4096,1024]{1,0:T(8,128)(2,1)} %wk_hbm.1, bf16[4096,1024]{1,0:T(8,128)(2,1)} %wv_hbm.1, f32[16,1,320]{2,1,0:T(1,128)} %copy-done, ...), custom_call_target="tpu_custom_call" | custom-call | tf_op jit(solution)/shard_map/pallas_call | solution.py:671
  175.3 0.9 slice_reduce_fusion
  176.3 3.6 %multiply_convert_fusion = (bf16[128,4096]{1,0:T(8,128)(2,1)}, bf16[128,4096]{1,0:T(8,128)(2,1)}) fusion(f32[4096]{0:T(1024)S(1)} %convert_element_type.22, f32[128]{0:T(128)S(1)} %slice_reduce_fusion, f32[128,4096]{1,0:T(8,128)} %get-tuple-element.4, bf16[128,4096]{1,0:T(8,128)(2,1)} %tok_ref.1), kind=kLoop, calls=%fused_computation | loop fusion | flops 3670016 | bytes 5259776 | tf_op jit(solution)/shard_map/convert_element_type | solution.py:746
  (17 shorter events, 0.2 us)
Async XLA Ops:
  3.6 1.4 copy-start

commit v4 on v3

--- a/solution.py
+++ b/solution.py
@@ -13,10 +13,10 @@
 EPS = 1e-05
 TILE = 256
 WIDE = 512
-SKEW = 3
+SKEW = 4
 SPREAD_SKEW = 3
 LEVELS = 32766.0
-FORWARD = 2
+FORWARD = 3
 RING = 4
 DEEP = 8
 F32 = jnp.float32
@@ -140,11 +140,7 @@
 
 def plan(n, chips, tiles, wides):
     units = tiles + 1
-    start = 0
-    for p in range(chips):
-        g = (p + 1) % chips
-        start = max(start, (g + 1) * units + SKEW * (n - 1) - p * tiles)
-    start = max(start, (chips - 1) * units + SKEW * (n - 1) + 1)
+    start = (chips - 1) * units + SKEW * (n - 1)
     lag = max(0, tiles - wides) * chips + tiles + SPREAD_SKEW * (n - 1)
     return start, lag
 
@@ -177,6 +173,8 @@
     right, left = jnp.minimum(me + 1, last), jnp.maximum(me - 1, 0)
     end_row = jnp.where(me == last, 1, 0)
     is_end = (me == 0) | (me == last)
+    relay = chips == 4
+    order = ([1, chips - 1] + list(range(2, chips - 1)))[: chips - 1] + [0]
 
     def w_copies(u):
         if u == 0:
@@ -246,7 +244,7 @@
         def _(i):
             at = pl.ds(pl.multiple_of(i * 16, 16), 16)
             x = tok[g, at, :].astype(F32)
-            scaled[at, :] = (x * gain_ref[...].astype(F32)).astype(BF16)
+            scaled[at, :] = (x * jnp.broadcast_to(gain_ref[...].astype(F32).reshape(1, -1), x.shape)).astype(BF16)
             sqp[at, :] = fold_lanes(x * x)
 
         for e in range(2):
@@ -383,7 +381,9 @@
                 copy.wait_send()
 
     def group(p):
-        return lax.rem(p + 1, chips)
+        return jnp.where(
+            p == chips - 1, 0, jnp.where(p == 0, 1, jnp.where(p == 1, chips - 1, p))
+        )
 
     def row_scale(k):
         return column(lax.rsqrt(sqs[pl.ds(k, 1), :] / all_width + EPS))
@@ -511,7 +511,10 @@
         return tok.at[p, pl.ds(part * hrows, hrows), at]
 
     def peer_copy(v, part):
-        m, _ = member(group(lax.div(v, wides)), part, chips)
+        g = group(lax.div(v, wides))
+        m, _ = member(g, part, chips)
+        if relay and part == 1:
+            m = jnp.where(g == chips - 1, 1 + core, m)
         return send_to(
             stage(v, part), land(v, part), xsem, (v, part), ha=mirror(chip, m, chips) * 2 + core
         )
@@ -561,7 +564,17 @@
         @pl.when(p < chips - 1)
         def _():
             for part in range(2):
-                stage(v, part)[...] = both[part * hrows : (part + 1) * hrows].astype(BF16)
+                extra = stage(v, part)
+                extra[...] = both[part * hrows : (part + 1) * hrows].astype(BF16)
+                if relay:
+                    through = wides + k
+
+                    @pl.when((group(p) == chips - 2) & (part == 1 - core))
+                    def _():
+                        peer_copy(through, 1).wait_recv()
+                        here = both[part * hrows : (part + 1) * hrows]
+                        extra[...] = (here + land(through, 1)[...].astype(F32)).astype(BF16)
+
                 peer_copy(v, part).start()
 
         @pl.when(p == chips - 1)
@@ -603,8 +616,10 @@
     def _(k):
         halves = [own[k, pl.ds(f * hrows, hrows), :] for f in range(2)]
         for p in range(chips - 1):
-            g, v = p + 1, p * wides + k
+            g, v = order[p], p * wides + k
             for part in range(2):
+                if relay and g == chips - 1 and part == 1:
+                    continue
                 peer_copy(v, part).wait_recv()
                 f = part if g == chips - 1 else (g - 1) % 2
                 halves[f] = halves[f] + land(v, part)[...].astype(F32)
@@ -737,7 +752,7 @@
         [padded[None, k * half : (k + 1) * half + WINDOW] for k in range(2 * n_ha)]
     )
     attended, scale_two = layer(
-        tokens, gain_attn.reshape(1, width), w_query, w_key, w_value, seg_rows, rope_rows(),
+        tokens, gain_attn, w_query, w_key, w_value, seg_rows, rope_rows(),
         w_out, n_wa, n_ha,
     )
     residual_out = (tokens.astype(F32) + attended).astype(BF16)

time: 180 us -> 169 us (0.939)
  Pallas kernels: 170 us -> 160 us
    pallas_call x1, Pallas kernels: 170 us -> 160 us  [layer(): pl.pallas_call(functools.partial(layer_kernel, n, chips, rows, tiles, wid...]
where the time goes in v4:
time: 169 us
  Pallas kernels  160 us (95%)
  other arithmetic  6.42 us (4%)
    pallas_call x1, Pallas kernels, layer(): pl.pallas_call(functools.partial(layer_kernel, n, chips, rows, tiles, wid...  160 us
    convert_element_type x1, other arithmetic, on_device(): ffn_input = (residual_out.astype(F32) * scale_two[:, :1] * gain_ffn.astyp...  3.63 us

profile of v4, /device:TPU:0, one launch (start us, length us, event | category | flops | bytes accessed | tf_op | source)
XLA Modules:
  0.0 168.6 jit_solution(444639604036071733)
XLA Ops:
  0.6 0.7 pad_convert_fusion
  1.3 0.7 convert_element_type.22
  2.0 0.1 fusion.3
  2.3 0.0 copy-start
  2.3 0.5 fusion.1
  2.8 0.9 pad_maximum_fusion.rope_ref
  3.7 0.0 copy-done
  3.7 160.3 %shard_map.95 = (f32[128,4096]{1,0:T(8,128)}, f32[128,128]{1,0:T(8,128)}) custom-call(bf16[128,4096]{1,0:T(8,128)(2,1)} %tok_ref.1, bf16[4096]{0:T(1024)(128)(2,1)} %gain_ref.1, bf16[4096,2048]{1,0:T(8,128)(2,1)} %wq_hbm.1, bf16[4096,1024]{1,0:T(8,128)(2,1)} %wk_hbm.1, bf16[4096,1024]{1,0:T(8,128)(2,1)} %wv_hbm.1, f32[16,1,320]{2,1,0:T(1,128)} %copy-done, ...), custom_call_target="tpu_custom_call" | custom-call | tf_op jit(solution)/shard_map/pallas_call | solution.py:686
  164.1 0.9 slice_reduce_fusion
  165.0 3.6 %multiply_convert_fusion = (bf16[128,4096]{1,0:T(8,128)(2,1)}, bf16[128,4096]{1,0:T(8,128)(2,1)}) fusion(f32[4096]{0:T(1024)S(1)} %convert_element_type.22, f32[128]{0:T(128)S(1)} %slice_reduce_fusion, f32[128,4096]{1,0:T(8,128)} %get-tuple-element.4, bf16[128,4096]{1,0:T(8,128)(2,1)} %tok_ref.1), kind=kLoop, calls=%fused_computation | loop fusion | flops 3670016 | bytes 5259776 | tf_op jit(solution)/shard_map/convert_element_type | solution.py:761
  (17 shorter events, 0.2 us)
Async XLA Ops:
  2.3 1.4 copy-start

commit v5 on v4

--- a/solution.py
+++ b/solution.py
@@ -141,7 +141,7 @@
 def plan(n, chips, tiles, wides):
     units = tiles + 1
     start = (chips - 1) * units + SKEW * (n - 1)
-    lag = max(0, tiles - wides) * chips + tiles + SPREAD_SKEW * (n - 1)
+    lag = max(0, tiles - wides) * chips + tiles - 1 + SPREAD_SKEW * (n - 1)
     return start, lag
 
 

time: 169 us -> 167 us (0.988)
  no operation moved by 1% of the time
where the time goes in v5:
time: 167 us
  Pallas kernels  159 us (95%)
  other arithmetic  6.42 us (4%)
    pallas_call x1, Pallas kernels, layer(): pl.pallas_call(functools.partial(layer_kernel, n, chips, rows, tiles, wid...  159 us
    convert_element_type x1, other arithmetic, on_device(): ffn_input = (residual_out.astype(F32) * scale_two[:, :1] * gain_ffn.astyp...  3.63 us

profile of v5, /device:TPU:0, one launch (start us, length us, event | category | flops | bytes accessed | tf_op | source)
XLA Modules:
  0.0 166.9 jit_solution(12224647554263706313)
XLA Ops:
  0.6 0.7 pad_convert_fusion
  1.3 0.7 convert_element_type.22
  2.0 0.1 fusion.3
  2.3 0.0 copy-start
  2.3 0.5 fusion.1
  2.8 0.9 pad_maximum_fusion.rope_ref
  3.7 0.0 copy-done
  3.7 158.7 %shard_map.95 = (f32[128,4096]{1,0:T(8,128)}, f32[128,128]{1,0:T(8,128)}) custom-call(bf16[128,4096]{1,0:T(8,128)(2,1)} %tok_ref.1, bf16[4096]{0:T(1024)(128)(2,1)} %gain_ref.1, bf16[4096,2048]{1,0:T(8,128)(2,1)} %wq_hbm.1, bf16[4096,1024]{1,0:T(8,128)(2,1)} %wk_hbm.1, bf16[4096,1024]{1,0:T(8,128)(2,1)} %wv_hbm.1, f32[16,1,320]{2,1,0:T(1,128)} %copy-done, ...), custom_call_target="tpu_custom_call" | custom-call | tf_op jit(solution)/shard_map/pallas_call | solution.py:686
  162.4 0.9 slice_reduce_fusion
  163.3 3.6 %multiply_convert_fusion = (bf16[128,4096]{1,0:T(8,128)(2,1)}, bf16[128,4096]{1,0:T(8,128)(2,1)}) fusion(f32[4096]{0:T(1024)S(1)} %convert_element_type.22, f32[128]{0:T(128)S(1)} %slice_reduce_fusion, f32[128,4096]{1,0:T(8,128)} %get-tuple-element.4, bf16[128,4096]{1,0:T(8,128)(2,1)} %tok_ref.1), kind=kLoop, calls=%fused_computation | loop fusion | flops 3670016 | bytes 5259776 | tf_op jit(solution)/shard_map/convert_element_type | solution.py:761
  (17 shorter events, 0.2 us)
Async XLA Ops:
  2.3 1.4 copy-start

commit v6 on v5

--- a/solution.py
+++ b/solution.py
@@ -581,6 +581,17 @@
         def _():
             own[k] = both
 
+    def spread_drain(j):
+        @pl.when(me < last)
+        def _():
+            spread_copy(j, 0, right, srsem).wait_send()
+
+        @pl.when(me > 0)
+        def _():
+            spread_copy(j, 1, left, slsem).wait_send()
+
+    drained, spent = min(count, lag + n_unit + 1), min(n_chunk, n_unit)
+
     @pl.loop(0, start + lag + n_unit + 1)
     def _(s):
         @pl.when(s < count + SKEW * last)
@@ -603,6 +614,15 @@
             spread_step(r, last - me, left, 1, slsem)
 
         v = r - lag
+
+        @pl.when((r >= 0) & (r < drained))
+        def _():
+            drain(r, me, right, qr, kr, er, rsem, resem)
+            drain(r, last - me, left, ql, kl, el, lsem, lesem)
+
+        @pl.when((v >= 0) & (v < spent))
+        def _():
+            spread_drain(v)
 
         @pl.when((v >= 0) & (v < n_unit))
         def _():
@@ -641,20 +661,14 @@
     for copy in small_two:
         copy.start()
 
-    @pl.loop(0, count)
+    @pl.loop(drained, count)
     def _(j):
         drain(j, me, right, qr, kr, er, rsem, resem)
         drain(j, last - me, left, ql, kl, el, lsem, lesem)
 
-    @pl.loop(0, n_chunk)
+    @pl.loop(spent, n_chunk)
     def _(j):
-        @pl.when(me < last)
-        def _():
-            spread_copy(j, 0, right, srsem).wait_send()
-
-        @pl.when(me > 0)
-        def _():
-            spread_copy(j, 1, left, slsem).wait_send()
+        spread_drain(j)
 
     @pl.loop(0, n_unit - wides)
     def _(v):

time: 167 us -> 168 us (level)
  no operation moved by 1% of the time
where the time goes in v6:
time: 168 us; the launch traced here: 167 us
  Pallas kernels  159 us (95%)
  other arithmetic  6.42 us (4%)
    pallas_call x1, Pallas kernels, layer(): pl.pallas_call(functools.partial(layer_kernel, n, chips, rows, tiles, wid...  159 us
    convert_element_type x1, other arithmetic, on_device(): ffn_input = (residual_out.astype(F32) * scale_two[:, :1] * gain_ffn.astyp...  3.63 us

profile of v6, /device:TPU:0, one launch (start us, length us, event | category | flops | bytes accessed | tf_op | source)
XLA Modules:
  0.0 167.5 jit_solution(4048453563826438529)
XLA Ops:
  0.6 0.7 pad_convert_fusion
  1.3 0.7 convert_element_type.22
  2.0 0.1 fusion.3
  2.3 0.0 copy-start
  2.3 0.5 fusion.1
  2.8 0.9 pad_maximum_fusion.rope_ref
  3.7 0.0 copy-done
  3.7 159.2 %shard_map.95 = (f32[128,4096]{1,0:T(8,128)}, f32[128,128]{1,0:T(8,128)}) custom-call(bf16[128,4096]{1,0:T(8,128)(2,1)} %tok_ref.1, bf16[4096]{0:T(1024)(128)(2,1)} %gain_ref.1, bf16[4096,2048]{1,0:T(8,128)(2,1)} %wq_hbm.1, bf16[4096,1024]{1,0:T(8,128)(2,1)} %wk_hbm.1, bf16[4096,1024]{1,0:T(8,128)(2,1)} %wv_hbm.1, f32[16,1,320]{2,1,0:T(1,128)} %copy-done, ...), custom_call_target="tpu_custom_call" | custom-call | tf_op jit(solution)/shard_map/pallas_call | solution.py:700
  162.9 0.9 slice_reduce_fusion
  163.8 3.6 %multiply_convert_fusion = (bf16[128,4096]{1,0:T(8,128)(2,1)}, bf16[128,4096]{1,0:T(8,128)(2,1)}) fusion(f32[4096]{0:T(1024)S(1)} %convert_element_type.22, f32[128]{0:T(128)S(1)} %slice_reduce_fusion, f32[128,4096]{1,0:T(8,128)} %get-tuple-element.4, bf16[128,4096]{1,0:T(8,128)(2,1)} %tok_ref.1), kind=kLoop, calls=%fused_computation | loop fusion | flops 3670016 | bytes 5259776 | tf_op jit(solution)/shard_map/convert_element_type | solution.py:775
  (17 shorter events, 0.2 us)
Async XLA Ops:
  2.3 1.4 copy-start
